TPU v7x, 256 devices: a whole 4x4x8 slice. The times are simulated.
256 devices in a mesh: peer: 32 (over z, y_hi, core), grp: 8 (over y_lo, x).
Axes of the slice: x: 4, y: 4 (y_hi: 2, y_lo: 2; y = y_hi * 2 + y_lo), z: 8, core: 2. Of those that a mesh axis runs over, the one named last changes fastest.
Arguments:
- images: bfloat16 [2, 32, 8, 8, 32, 384], P(None, 'peer', 'grp'), may hold values from -6 to 6
- cotangent: bfloat16 [2, 32, 8, 8, 32, 384], P(None, 'peer', 'grp'), may hold values from -6 to 6
- dw_kernel: float32 [32, 49, 384], P('peer', None, 'grp'), may hold values from -0.875 to 0.875
- chan_vec: float32 [32, 5, 384], P('peer', None, 'grp'), may hold values from 0.25 to 1.5
- w_in: float32 [32, 384, 1536], P('peer', 'grp'), may hold values from -0.3125 to 0.3125
- b_in: float32 [32, 1536], P('peer', 'grp'), may hold values from -3 to 3
- w_out: float32 [32, 1536, 384], P('peer', 'grp'), may hold values from -0.15625 to 0.15625
- mom_kernel: float32 [32, 49, 384], P('peer', None, 'grp'), may hold values from -300 to 300
- mom_chan: float32 [32, 5, 384], P('peer', None, 'grp'), may hold values from -300 to 300
- mom_in: float32 [32, 384, 1536], P('peer', 'grp'), may hold values from -300 to 300
- mom_bin: float32 [32, 1536], P('peer', 'grp'), may hold values from -300 to 300
- mom_out: float32 [32, 1536, 384], P('peer', 'grp'), may hold values from -300 to 300
Outputs:
- new_kernel: float32 [32, 49, 384], P('peer', None, 'grp')
- new_chan: float32 [32, 5, 384], P('peer', None, 'grp')
- new_in: float32 [32, 384, 1536], P('peer', 'grp')
- new_bin: float32 [32, 1536], P('peer', 'grp')
- new_out: float32 [32, 1536, 384], P('peer', 'grp')
- features: bfloat16 [32, 8, 8, 32, 384], P('peer', 'grp')
All inputs are finite; a program needn't handle non-finite values.
Results may differ from a plain program's by a relative error of at most 0.01.
Values may be sent and summed in bfloat16 or wider, within the bound.
No kernel may reach another device: no remote copies, remote signals or barrier semaphores. Data moves between devices by JAX's collectives and lax.ppermute only.
A program may use at most 64 MiB of HBM per device.

v0:
```python
import functools

import jax
import jax.numpy as jnp
from jax import lax
from jax.experimental import pallas as pl
from jax.experimental.pallas import tpu as pltpu
from jax.sharding import PartitionSpec as P


STEPS = 2
EPS = 1e-06
MOMENTUM = 0.9
RATE = 0.0005
SQRT_HALF = 0.7071067811865476
INV_ROOT_TWO_PI = 0.3989422804014327


RING = 4
PAIR = 2
HEIGHT, WIDTH, CHANNELS = 8, 32, 384
ROWS = HEIGHT * WIDTH
HIDDEN_PART = 384
BLOCK = 192
INNER = 48
TAPS = 49
PACKED = 2 * BLOCK + 16
SMALL = 56
LANES = 128
LIMIT = 9 * 2**20

F32 = jnp.float32
BF16 = jnp.bfloat16
VMEM = pl.BlockSpec(memory_space=pltpu.VMEM)
SMEM = pl.BlockSpec(memory_space=pltpu.SMEM)


def shift(block, k):
    route = [
        (y * RING + x, y * RING + (x + k) % RING) for y in range(PAIR) for x in range(RING)
    ]
    return lax.ppermute(block, "grp", route)


def swap(block):
    route = [(y * RING + x, (1 - y) * RING + x) for y in range(PAIR) for x in range(RING)]
    return lax.ppermute(block, "grp", route)


def pair_along(block, distance, flip):
    peers, members = lax.axis_size("peer"), PAIR * RING
    route = [
        (
            ((r - distance) % peers) * members + ((1 - y) if flip else y) * RING + x,
            r * members + y * RING + x,
        )
        for r in range(peers)
        for y in range(PAIR)
        for x in range(RING)
    ]
    return lax.ppermute(block, ("peer", "grp"), route)


def passed_along(block, distance):
    count = lax.axis_size("peer")
    return lax.ppermute(block, "peer", [((i - distance) % count, i) for i in range(count)])


def ring_order(slots, x):
    a, b, c, d = slots
    return lax.dynamic_slice_in_dim(jnp.stack([d, c, b, a, d, c, b]), RING - 1 - x, RING, 0)


def fill_padded(refs, pad):
    for k, ref in enumerate(refs):
        rows = pl.ds(k * HEIGHT, HEIGHT)
        pad[rows, 0:8, :] = jnp.zeros((HEIGHT, 8, CHANNELS), F32)
        pad[rows, 8 : 8 + WIDTH, :] = (
            ref[0:ROWS, :].astype(F32).reshape(HEIGHT, WIDTH, CHANNELS)
        )
        pad[rows, 8 + WIDTH : 16 + WIDTH, :] = jnp.zeros((HEIGHT, 8, CHANNELS), F32)


def fill_shifted(pad, base, lanes, shifted):
    for j in range(7):
        for h in range(HEIGHT):
            shifted[j * HEIGHT + h] = pad[base + h, 5 + j : 5 + j + WIDTH, lanes]


def front_kernel(i0, i1, i2, i3, small, normed, scaled, spread, pad, conv, shifted):
    fill_padded((i0, i1, i2, i3), pad)

    def tile(t, carry):
        image = t // 3
        lanes = pl.ds(pl.multiple_of((t % 3) * LANES, LANES), LANES)
        base = image * HEIGHT
        bias = small[TAPS : TAPS + 1, lanes]
        fill_shifted(pad, base, lanes, shifted)
        for wt in range(WIDTH // 8):
            acc = [jnp.broadcast_to(bias, (8, LANES)) for _ in range(HEIGHT)]
            for j in range(7):
                at = slice(8 * wt, 8 * wt + 8)
                src = [shifted[j * HEIGHT + h, at, :] for h in range(HEIGHT)]
                for i in range(7):
                    tap = small[7 * i + j : 7 * i + j + 1, lanes]
                    for h in range(HEIGHT):
                        s = h + i - 3
                        if 0 <= s < HEIGHT:
                            acc[h] = acc[h] + tap * src[s]
            for h in range(HEIGHT):
                conv[(base + h) * 4 + wt, :, lanes] = acc[h]
        return carry

    lax.fori_loop(0, RING * 3, tile, 0)
    gain = small[TAPS + 1 : TAPS + 2, :]
    offset = small[TAPS + 2 : TAPS + 3, :]

    def norm(c, carry):
        v = conv[pl.ds(c * 8, 8), :, :].reshape(64, CHANNELS)
        rows = pl.ds(pl.multiple_of(c * 64, 64), 64)
        center = v - jnp.sum(v, axis=-1, keepdims=True) * (1.0 / CHANNELS)
        var = jnp.sum(center * center, axis=-1, keepdims=True) * (1.0 / CHANNELS)
        inv = lax.rsqrt(var + EPS)
        sc = center * inv
        scaled[rows, :] = sc
        spread[rows, :] = jnp.broadcast_to(inv, (64, LANES))
        normed[rows, :] = (sc * gain + offset).astype(BF16)
        return carry

    lax.fori_loop(0, RING * ROWS // 64, norm, 0)


def front(images, small):
    total = RING * ROWS
    return pl.pallas_call(
        front_kernel,
        out_shape=(
            jax.ShapeDtypeStruct((total, CHANNELS), BF16),
            jax.ShapeDtypeStruct((total, CHANNELS), F32),
            jax.ShapeDtypeStruct((total, LANES), F32),
        ),
        in_specs=[VMEM] * 5,
        out_specs=(VMEM,) * 3,
        scratch_shapes=[
            pltpu.VMEM((RING * HEIGHT, WIDTH + 16, CHANNELS), F32),
            pltpu.VMEM((RING * HEIGHT * 4, 8, CHANNELS), F32),
            pltpu.VMEM((7 * HEIGHT, WIDTH, LANES), F32),
        ],
        cost_estimate=pl.CostEstimate(flops=10**9, transcendentals=0, bytes_accessed=30 * 10**6),
        compiler_params=pltpu.CompilerParams(vmem_limit_bytes=LIMIT),
        name="front",
    )(*images, small)


def contract(a, b, da, db):
    return lax.dot_general(a, b, (((da,), (db,)), ((), ())), preferred_element_type=F32)


def mlp_kernel(
    last, y_ref, normed, own, other, b_ref, c0, c1, c2, c3, small, *refs
):
    g_own, g_send, dnormed, aux = refs[:4]
    partial = refs[4:8] if last else ()
    w_in, w_out, acc_out, acc_in, cots = refs[-5:]
    y = y_ref[0]
    mine = pl.ds(pl.multiple_of(y * BLOCK, 64), BLOCK)
    theirs = pl.ds(pl.multiple_of((1 - y) * BLOCK, 64), BLOCK)
    w_out[mine, :] = own[0:BLOCK, :]
    w_out[theirs, :] = other[0:BLOCK, :]
    w_in[mine, :] = own[BLOCK : 2 * BLOCK, :]
    w_in[theirs, :] = other[BLOCK : 2 * BLOCK, :]
    bias = b_ref[...]
    b_out = small[TAPS + 3 : TAPS + 4, :]
    scale = small[TAPS + 4 : TAPS + 5, :]
    top = c0.shape[0] - ROWS
    for k, c_ref in enumerate((c0, c1, c2, c3)):
        cots[k] = c_ref[top:, :]
    acc_out[...] = jnp.zeros_like(acc_out)
    acc_in[...] = jnp.zeros_like(acc_in)

    def image(k, sums):
        c_sum, g_bin = sums
        rows = pl.ds(pl.multiple_of(k * ROWS, ROWS), ROWS)
        nrm = normed[rows, :]
        cot = cots[k]
        wide = cot.astype(F32)
        pre = contract(nrm, w_in[...], 1, 0) + bias
        phi = 0.5 * (1.0 + lax.erf(pre * SQRT_HALF))
        hidden = (pre * phi).astype(BF16)
        slope = phi + pre * jnp.exp(-0.5 * pre * pre) * INV_ROOT_TWO_PI
        dmlp = (wide * scale).astype(BF16)
        dpre = (contract(dmlp, w_out[...], 1, 1) * slope).astype(BF16)
        dnormed[rows, :] = contract(dpre, w_in[...], 1, 1)
        acc_out[...] += contract(hidden, cot, 0, 0)
        acc_in[...] += contract(nrm, dpre, 0, 0)
        if last:
            product = contract(hidden, w_out[...], 1, 0).astype(BF16)
            for n in range(RING):

                @pl.when(k == n)
                def _():
                    partial[n][...] = product

        return (
            c_sum + jnp.sum(wide, axis=0, keepdims=True),
            g_bin + jnp.sum(dpre.astype(F32), axis=0, keepdims=True),
        )

    zero_row = jnp.zeros((1, CHANNELS), F32)
    c_sum, g_bin = lax.fori_loop(0, RING, image, (zero_row, zero_row))
    share = 1.0 / RING
    scale_grad = jnp.sum(w_out[...].astype(F32) * acc_out[...], axis=0, keepdims=True)
    aux[0:1, :] = share * (scale * c_sum)
    aux[1:2, :] = scale_grad + share * (b_out * c_sum)
    g_own[0:BLOCK, :] = acc_out[mine, :] * scale
    g_send[0:BLOCK, :] = (acc_out[theirs, :] * scale).astype(BF16)
    g_own[BLOCK : 2 * BLOCK, :] = acc_in[mine, :]
    g_send[BLOCK : 2 * BLOCK, :] = acc_in[theirs, :].astype(BF16)
    first = lax.broadcasted_iota(jnp.int32, (16, HIDDEN_PART), 0) == 0
    half = (lax.broadcasted_iota(jnp.int32, (16, HIDDEN_PART), 1) >= BLOCK).astype(jnp.int32)
    block = jnp.broadcast_to(g_bin, (16, HIDDEN_PART))
    zero = jnp.zeros_like(block)
    g_own[2 * BLOCK :, :] = jnp.where(first & (half == y), block, zero)
    g_send[2 * BLOCK :, :] = jnp.where(first & (half != y), block, zero).astype(BF16)


def mlp(last, y, normed, own, other, bias, cots, small):
    total = RING * ROWS
    shapes = [
        jax.ShapeDtypeStruct((PACKED, CHANNELS), F32),
        pltpu.HBM((PACKED, CHANNELS), BF16),
        jax.ShapeDtypeStruct((total, CHANNELS), F32),
        jax.ShapeDtypeStruct((8, CHANNELS), F32),
    ]
    if last:
        shapes += [pltpu.HBM((ROWS, CHANNELS), BF16)] * RING
    return pl.pallas_call(
        functools.partial(mlp_kernel, last),
        out_shape=tuple(shapes),
        in_specs=[SMEM] + [VMEM] * 9,
        out_specs=(VMEM,) * len(shapes),
        scratch_shapes=[
            pltpu.VMEM((CHANNELS, HIDDEN_PART), BF16),
            pltpu.VMEM((HIDDEN_PART, CHANNELS), BF16),
            pltpu.VMEM((HIDDEN_PART, CHANNELS), F32),
            pltpu.VMEM((CHANNELS, HIDDEN_PART), F32),
            pltpu.VMEM((RING, ROWS, CHANNELS), BF16),
        ],
        cost_estimate=pl.CostEstimate(
            flops=2 * 10**9, transcendentals=10**6, bytes_accessed=20 * 10**6
        ),
        compiler_params=pltpu.CompilerParams(vmem_limit_bytes=LIMIT),
        name="mlp",
    )(y, normed, own, other, bias, *cots, small)


def back_kernel(start, count, final, *refs):
    photos, refs = refs[:count], refs[count:]
    scaled, spread, dnormed, small, extra, out = refs[:6]
    pad, dconv, taps, rows_out, shifted = refs[6:]
    fill_padded(photos, pad)
    gain = small[TAPS + 1 : TAPS + 2, :]
    zero = jnp.zeros((8, CHANNELS), F32)

    def norm(c, sums):
        bias_sum, gain_sum, shift_sum = sums
        rows = pl.ds(pl.multiple_of(start * ROWS + c * 64, 64), 64)
        sc = scaled[rows, :]
        dn = dnormed[rows, :]
        inv = spread[rows, 0:1]
        ds = dn * gain
        mean = jnp.sum(ds, axis=-1, keepdims=True) * (1.0 / CHANNELS)
        along = jnp.sum(ds * sc, axis=-1, keepdims=True) * (1.0 / CHANNELS)
        dc = (inv * (ds - mean - sc * along)).reshape(8, 8, CHANNELS)
        dconv[pl.ds(c * 8, 8), :, :] = dc
        return (
            bias_sum + jnp.sum(dc, axis=0),
            gain_sum + jnp.sum((dn * sc).reshape(8, 8, CHANNELS), axis=0),
            shift_sum + jnp.sum(dn.reshape(8, 8, CHANNELS), axis=0),
        )

    sums = lax.fori_loop(0, count * ROWS // 64, norm, (zero, zero, zero))
    taps[...] = jnp.zeros_like(taps)

    def tile(t, carry):
        image = t // 3
        lanes = pl.ds(pl.multiple_of((t % 3) * LANES, LANES), LANES)
        base = image * HEIGHT
        fill_shifted(pad, base, lanes, shifted)
        for j in range(7):
            acc = [taps[7 * i + j, :, lanes] for i in range(7)]
            for wt in range(WIDTH // 8):
                at = slice(8 * wt, 8 * wt + 8)
                src = [shifted[j * HEIGHT + h, at, :] for h in range(HEIGHT)]
                grad = [dconv[(base + h) * 4 + wt, :, lanes] for h in range(HEIGHT)]
                for i in range(7):
                    for h in range(HEIGHT):
                        s = h + i - 3
                        if 0 <= s < HEIGHT:
                            acc[i] = acc[i] + grad[h] * src[s]
            for i in range(7):
                taps[7 * i + j, :, lanes] = acc[i]
        return carry

    lax.fori_loop(0, count * 3, tile, 0)
    rows_out[0:TAPS, :] = jnp.sum(taps[...], axis=1)
    for r, value in enumerate(sums):
        rows_out[TAPS + r : TAPS + r + 1, :] = jnp.sum(value, axis=0, keepdims=True)
    rows_out[TAPS + 3 : SMALL, :] = jnp.zeros((SMALL - TAPS - 3, CHANNELS), F32)
    if start == 0:
        rows_out[TAPS + 3 : TAPS + 5, :] = extra[0:2, :]
        total = rows_out[...]
    else:
        total = rows_out[...] + extra[...]
    out[...] = total.astype(BF16) if final else total


def back(start, final, photos, scaled, spread, dnormed, small, extra):
    count = len(photos)
    return pl.pallas_call(
        functools.partial(back_kernel, start, count, final),
        out_shape=jax.ShapeDtypeStruct((SMALL, CHANNELS), BF16 if final else F32),
        in_specs=[VMEM] * (count + 5),
        out_specs=VMEM,
        scratch_shapes=[
            pltpu.VMEM((count * HEIGHT, WIDTH + 16, CHANNELS), F32),
            pltpu.VMEM((count * HEIGHT * 4, 8, CHANNELS), F32),
            pltpu.VMEM((TAPS, 8, CHANNELS), F32),
            pltpu.VMEM((SMALL, CHANNELS), F32),
            pltpu.VMEM((7 * HEIGHT, WIDTH, LANES), F32),
        ],
        cost_estimate=pl.CostEstimate(
            flops=10**9, transcendentals=0, bytes_accessed=count * 8 * 10**6
        ),
        compiler_params=pltpu.CompilerParams(vmem_limit_bytes=LIMIT),
        name="back",
    )(*photos, scaled, spread, dnormed, small, extra)


def per_device(
    images,
    cotangent,
    dw_kernel,
    chan_vec,
    w_in,
    b_in,
    w_out,
    mom_kernel,
    mom_chan,
    mom_in,
    mom_bin,
    mom_out,
):
    member = lax.axis_index("grp")
    y, x = member // RING, member % RING
    y_scalar = y.astype(jnp.int32).reshape(1)
    photos = [images[s, 0, 0].reshape(ROWS, CHANNELS) for s in range(STEPS)]
    cots = [cotangent[s, 0, 0].reshape(ROWS, CHANNELS) for s in range(STEPS)]

    tiny = jnp.concatenate(
        [
            jnp.concatenate([dw_kernel[0], chan_vec[0]], axis=0),
            jnp.concatenate([mom_kernel[0], mom_chan[0]], axis=0),
        ],
        axis=1,
    )
    from_pair = swap(tiny)
    couple = jnp.concatenate(
        [jnp.where(y == 0, tiny, from_pair), jnp.where(y == 0, from_pair, tiny)], axis=1
    )
    couple = jnp.pad(couple, ((0, SMALL - TAPS - 5), (0, 0)))
    couple_high = lax.reduce_precision(couple, 8, 7)
    couple_low = couple - couple_high
    couple_rows = jnp.concatenate([couple_high, couple_low], axis=1).astype(BF16)

    low = jnp.concatenate([w_in[0], mom_in[0]], axis=0).astype(BF16)

    def columns(k):
        at = ((x + k) % RING) * BLOCK
        left = lax.dynamic_slice_in_dim(low, at, BLOCK, 1)
        right = lax.dynamic_slice_in_dim(low, at + RING * BLOCK, BLOCK, 1)
        return jnp.concatenate([left, right], axis=1)

    packs = [
        jnp.concatenate([photos[0], columns(k), couple_rows], axis=0) for k in range(1, RING)
    ]
    came = [shift(packs[k - 1], k) for k in range(1, RING)]
    arrived = [photos[0]] + came
    couples = [couple_rows] + [c[ROWS + 2 * INNER :] for c in came]
    whole = ring_order(couples, x).astype(F32)
    whole = (whole[:, :, : 4 * INNER] + whole[:, :, 4 * INNER :]).reshape(
        RING, SMALL, PAIR, 2, INNER
    )
    whole = whole.transpose(3, 1, 2, 0, 4).reshape(2, SMALL, CHANNELS)
    small, small_m = whole[0], whole[1]

    tiles = ring_order([columns(0)] + [c[ROWS : ROWS + 2 * INNER] for c in came], x)
    tiles = tiles.astype(F32)
    in_share = tiles[:, :INNER].reshape(BLOCK, HIDDEN_PART)
    in_mom = tiles[:, INNER:].reshape(BLOCK, HIDDEN_PART)
    half = (jnp.arange(HIDDEN_PART) // BLOCK) == y

    def bias_rows(v):
        row = jnp.where(half, jnp.concatenate([v, v]), 0.0)[None]
        return jnp.pad(row, ((0, 15), (0, 0)))

    weights = jnp.concatenate([w_out[0], in_share, bias_rows(b_in[0])], axis=0)
    moments = jnp.concatenate([mom_out[0], in_mom, bias_rows(mom_bin[0])], axis=0)

    step_images = [arrived, None]
    step_cots = [[cots[0]] + [shift(cots[0], k) for k in range(1, RING)], None]
    later = jnp.concatenate([photos[1], cots[1]], axis=0)
    ahead = [later] + [shift(later, k) for k in range(1, RING)]
    step_images[1] = ahead
    step_cots[1] = ahead

    def columns_of(v, device):
        return lax.dynamic_slice(v, (0, device * INNER), (SMALL, INNER))

    features = None
    for step in range(STEPS):
        last = step == STEPS - 1
        base = small - (RATE * MOMENTUM) * small_m
        if last:
            base = columns_of(base, member)
        own = weights.astype(BF16)
        other = swap(own)
        normed, scaled, spread = front(step_images[step], small)
        bias = (weights[2 * BLOCK] + other[2 * BLOCK].astype(F32))[None]
        outs = mlp(last, y_scalar, normed, own, other, bias, step_cots[step], small)
        g_own, g_send, dnormed, aux = outs[:4]
        g_other = swap(g_send)
        saved = (scaled, spread, dnormed, small)
        shown = step_images[step]
        if last:
            early = back(0, False, shown[:2], *saved, aux)
            d_small = back(2, True, shown[2:], *saved, early)
        else:
            d_small = back(0, True, shown, *saved, aux)
        if last:
            parts = [outs[4]] + [shift(outs[4 + k], RING - k) for k in range(1, RING)]
            total = sum(p.astype(F32) for p in parts) + small[TAPS + 3]
            features = (photos[step].astype(F32) + small[TAPS + 4] * total).astype(BF16)
        moments = MOMENTUM * moments + (g_own + g_other.astype(F32))
        weights = weights - RATE * moments
        theirs = passed_along(weights.astype(BF16), 2**step)
        weights = 0.5 * (weights + theirs.astype(F32))
        rest = [shift(d_small, k) for k in range(1, RING)]
        half_sum = d_small.astype(F32) + sum(r.astype(F32) for r in rest)
        mine = theirs = half_sum.astype(BF16)
        if last:
            mine, theirs = columns_of(mine, member), columns_of(theirs, (1 - y) * RING + x)
        near = swap(theirs).astype(F32)
        part_step = base - RATE * mine.astype(F32)
        far_own = pair_along(part_step, 2**step, False)
        far_pair = pair_along(theirs, 2**step, True).astype(F32)
        grad = mine.astype(F32) + near
        small = 0.5 * ((base - RATE * grad) + (far_own - RATE * far_pair))
        small_m = MOMENTUM * small_m + grad if not last else None

    new_bin = lax.dynamic_slice_in_dim(weights[2 * BLOCK], y * BLOCK, BLOCK, 0)
    share = weights[BLOCK : 2 * BLOCK]

    def rows_for(k):
        return lax.dynamic_slice_in_dim(share, ((x + k) % RING) * INNER, INNER, 0)

    back_tiles = [rows_for(0)] + [shift(rows_for(k), k) for k in range(1, RING)]
    new_in = ring_order(back_tiles, x).reshape(RING, INNER, PAIR, BLOCK)
    new_in = new_in.transpose(1, 2, 0, 3).reshape(INNER, PAIR * RING * BLOCK)
    return (
        small[:TAPS][None],
        small[TAPS : TAPS + 5][None],
        new_in[None],
        new_bin[None],
        weights[:BLOCK][None],
        features.reshape(1, 1, HEIGHT, WIDTH, CHANNELS),
    )


def solution(mesh):
    return jax.shard_map(
        per_device,
        mesh=mesh,
        in_specs=(
            P(None, "peer", "grp", None, None, None),
            P(None, "peer", "grp", None, None, None),
            P("peer", None, "grp"),
            P("peer", None, "grp"),
            P("peer", "grp", None),
            P("peer", "grp"),
            P("peer", "grp", None),
            P("peer", None, "grp"),
            P("peer", None, "grp"),
            P("peer", "grp", None),
            P("peer", "grp"),
            P("peer", "grp", None),
        ),
        out_specs=(
            P("peer", None, "grp"),
            P("peer", None, "grp"),
            P("peer", "grp", None),
            P("peer", "grp"),
            P("peer", "grp", None),
            P("peer", "grp", None, None, None),
        ),
        check_vma=False,
    )
```

profile of v0, /device:TPU:8, one launch (start us, length us, event | category | flops | bytes accessed | tf_op | source)
XLA Modules:
  0.0 169.6 jit_solution(18205130142433220262)
XLA Ops:
  3.1 2.2 %collective-permute-start = (f32[54,96]{1,0:T(8,128)S(1)}, f32[54,96]{1,0:T(8,128)S(1)}, u32[]{:S(2)}, u32[]{:S(2)}) collective-permute-start(f32[54,96]{1,0:T(8,128)S(1)} %maximum_maximum_fusion), channel_id=1, source_target_pairs={{0,4},{1,5},{2,6},{3,7},{4,0},{5,1},{6,2},{7,3},{8,12},{9,13},{10,... | collective-permute-start | bytes 62216 | tf_op jit(solution)/shard_map/ppermute | solution.py:47
  5.3 1.7 %fusion.37 = (bf16[1,1,1,8,32,384]{5,4,3,2,1,0:T(8,128)(2,1)S(1)}, bf16[1,1,1,8,32,384]{5,4,3,2,1,0:T(8,128)(2,1)}) fusion(bf16[2,1,1,8,32,384]{5,4,3,2,1,0:T(8,128)(2,1)} %param.12), kind=kLoop, calls=%fused_computation.131 | loop fusion | bytes 786432 | tf_op jit(solution)/shard_map/slice | solution.py:357
  7.0 1.1 convert_bitcast_fusion
  9.0 1.1 collective-permute-start.1
  11.9 1.3 collective-permute-start.6
  13.2 1.4 collective-permute-start.7
  14.6 2.5 %collective-permute-start.2 = (bf16[408,384]{1,0:T(8,128)(2,1)S(1)}, bf16[408,384]{1,0:T(8,128)(2,1)S(1)}, u32[]{:S(2)}, u32[]{:S(2)}) collective-permute-start(bf16[408,384]{1,0:T(8,128)(2,1)S(1)} %get-tuple-element.99), channel_id=1, source_target_pairs={{0,2},{1,3},{2,0},{3,1},{4,6},{5,7},{6,4},{7,5},{8,10},{9,11},{10,... | collective-permute-start | bytes 940040 | tf_op jit(solution)/shard_map/ppermute | solution.py:42
  17.2 4.8 %collective-permute-done.1.i3.refs_3_ = bf16[408,384]{1,0:T(8,128)(2,1)S(1)} collective-permute-done((bf16[408,384]{1,0:T(8,128)(2,1)S(1)}, bf16[408,384]{1,0:T(8,128)(2,1)S(1)}, u32[]{:S(2)}, u32[]{:S(2)}) %collective-permute-start.1) | collective-permute-done | bytes 313376 | tf_op jit(solution)/shard_map/ppermute | solution.py:42
  22.0 8.1 %collective-permute-done.2.i2.refs_2_ = bf16[408,384]{1,0:T(8,128)(2,1)S(1)} collective-permute-done((bf16[408,384]{1,0:T(8,128)(2,1)S(1)}, bf16[408,384]{1,0:T(8,128)(2,1)S(1)}, u32[]{:S(2)}, u32[]{:S(2)}) %collective-permute-start.2) | collective-permute-done | bytes 313376 | tf_op jit(solution)/shard_map/ppermute | solution.py:42
  30.2 5.9 %collective-permute-done.3.i1.refs_1_ = bf16[408,384]{1,0:T(8,128)(2,1)S(1)} collective-permute-done((bf16[408,384]{1,0:T(8,128)(2,1)S(1)}, bf16[408,384]{1,0:T(8,128)(2,1)S(1)}, u32[]{:S(2)}, u32[]{:S(2)}) %collective-permute-start.3) | collective-permute-done | bytes 313376 | tf_op jit(solution)/shard_map/ppermute | solution.py:42
  37.9 1.6 collective-permute-start.4
  41.5 8.1 %front.2 = (bf16[1024,384]{1,0:T(8,128)(2,1)S(1)}, f32[1024,384]{1,0:T(8,128)S(1)}, f32[1024,128]{1,0:T(8,128)S(1)}) custom-call(bf16[256,384]{1,0:T(8,128)(2,1)S(1)} %bitcast.86, bf16[408,384]{1,0:T(8,128)(2,1)S(1)} %collective-permute-done.3.i1.refs_1_, bf16[408,384]{1,0:T(8,128)(2,1)S(1)} %collective-permute-done.2.i2.refs_2_, ...), custom_call_target="tpu_custom_call" | custom-call | flops 1000000000 | bytes 30000000 | tf_op jit(solution)/shard_map/front/pallas_call | solution.py:135
  51.3 5.7 %mlp.2 = (f32[400,384]{1,0:T(8,128)S(1)}, bf16[400,384]{1,0:T(8,128)(2,1)}, f32[1024,384]{1,0:T(8,128)S(1)}, f32[8,384]{1,0:T(8,128)S(1)}) custom-call(s32[1]{0:T(128)} %bitcast.13.y_ref, bf16[1024,384]{1,0:T(8,128)(2,1)S(1)} %get-tuple-element.26.normed, bf16[400,384]{1,0:T(8,128)(2,1)} %fusion.2.own, bf16[400,384]{1,0:T(8,128)(2,1)} %collective-permute-done.4.other, ...), custom_call_target="tpu_custom_call" | custom-call | flops 2000000000 | bytes 20000000 | tf_op jit(solution)/shard_map/mlp/pallas_call | solution.py:237
  58.3 1.0 copy.48
  62.3 1.0 copy-done.9
  63.4 7.5 %back.3 = bf16[56,384]{1,0:T(8,128)(2,1)S(1)} custom-call(bf16[256,384]{1,0:T(8,128)(2,1)S(1)} %bitcast.87, bf16[408,384]{1,0:T(8,128)(2,1)S(1)} %copy-done.5, bf16[408,384]{1,0:T(8,128)(2,1)S(1)} %copy-done.3, bf16[408,384]{1,0:T(8,128)(2,1)S(1)} %copy-done.1, f32[1024,384]{1,0:T(8,128)S(1)} %get-tuple-element.24.refs_4_, f32[1024,128]{1,0:T(8,128)S(1)} %copy-done.9, ...), custom_call_target="tpu_custom_call" | custom-call | flops 1000000000 | bytes 32000000 | tf_op jit(solution)/shard_map/back/pallas_call | solution.py:320
  71.0 2.0 %collective-permute-start.8 = (bf16[56,384]{1,0:T(8,128)(2,1)S(1)}, bf16[56,384]{1,0:T(8,128)(2,1)S(1)}, u32[]{:S(2)}, u32[]{:S(2)}) collective-permute-start(bf16[56,384]{1,0:T(8,128)(2,1)S(1)} %back.3), channel_id=1, source_target_pairs={{0,1},{1,2},{2,3},{3,0},{4,5},{5,6},{6,7},{7,4},{8,9},{9,10},{10,1... | collective-permute-start | bytes 129032 | tf_op jit(solution)/shard_map/ppermute | solution.py:42
  73.3 1.2 fusion.31
  75.3 1.2 collective-permute-done.8
  76.5 2.0 %collective-permute-done.9 = bf16[56,384]{1,0:T(8,128)(2,1)S(1)} collective-permute-done((bf16[56,384]{1,0:T(8,128)(2,1)S(1)}, bf16[56,384]{1,0:T(8,128)(2,1)S(1)}, u32[]{:S(2)}, u32[]{:S(2)}) %collective-permute-start.9) | collective-permute-done | bytes 43040 | tf_op jit(solution)/shard_map/ppermute | solution.py:42
  78.6 1.7 collective-permute-start.11
  81.0 2.1 %collective-permute-start.15 = (bf16[512,384]{1,0:T(8,128)(2,1)S(1)}, bf16[512,384]{1,0:T(8,128)(2,1)S(1)}, u32[]{:S(2)}, u32[]{:S(2)}) collective-permute-start(bf16[512,384]{1,0:T(8,128)(2,1)S(1)} %pad_maximum_fusion.i0.c0.refs_0_), channel_id=1, source_target_pairs={{0,3},{1,0},{2,1},{3,2},{4,7},{5,4},{6,5},{7,6},{8,11},{9,8},{10,9... | collective-permute-start | bytes 1179656 | tf_op jit(solution)/shard_map/ppermute | solution.py:42
  83.3 1.3 collective-permute-start.13
  84.6 1.2 collective-permute-done.18
  85.8 1.0 collective-permute-start.12
  86.9 1.1 fusion.33
  88.0 3.6 %collective-permute-done.13 = bf16[56,384]{1,0:T(8,128)(2,1)S(1)} collective-permute-done((bf16[56,384]{1,0:T(8,128)(2,1)S(1)}, bf16[56,384]{1,0:T(8,128)(2,1)S(1)}, u32[]{:S(2)}, u32[]{:S(2)}) %collective-permute-start.13) | collective-permute-done | bytes 43040 | tf_op jit(solution)/shard_map/ppermute | solution.py:61
  91.6 1.5 collective-permute-start.19
  94.3 5.7 %collective-permute-done.15.i3.c3.refs_1_ = bf16[512,384]{1,0:T(8,128)(2,1)S(1)} collective-permute-done((bf16[512,384]{1,0:T(8,128)(2,1)S(1)}, bf16[512,384]{1,0:T(8,128)(2,1)S(1)}, u32[]{:S(2)}, u32[]{:S(2)}) %collective-permute-start.15) | collective-permute-done | bytes 393248 | tf_op jit(solution)/shard_map/ppermute | solution.py:42
  100.5 8.1 %front.3 = (bf16[1024,384]{1,0:T(8,128)(2,1)S(1)}, f32[1024,384]{1,0:T(8,128)S(1)}, f32[1024,128]{1,0:T(8,128)S(1)}) custom-call(bf16[512,384]{1,0:T(8,128)(2,1)S(1)} %pad_maximum_fusion.i0.c0.refs_0_, bf16[512,384]{1,0:T(8,128)(2,1)S(1)} %collective-permute-done.16.i1.c1.refs_1_, bf16[512,384]{1,0:T(8,128)(2,1)S(1)} %collective-permute-done.14.i2.c2.refs_0_, ...), custom_call_target="tpu_custom_call" | custom-call | flops 1000000000 | bytes 30000000 | tf_op jit(solution)/shard_map/front/pallas_call | solution.py:135
  108.7 5.4 %mlp.3 = (f32[400,384]{1,0:T(8,128)S(1)}, bf16[400,384]{1,0:T(8,128)(2,1)}, f32[1024,384]{1,0:T(8,128)S(1)}, f32[8,384]{1,0:T(8,128)S(1)}, bf16[256,384]{1,0:T(8...) custom-call(s32[1]{0:T(128)} %bitcast.13.y_ref, ...), custom_call_target="tpu_custom_call" | custom-call | flops 2000000000 | bytes 20000000 | tf_op jit(solution)/shard_map/mlp/pallas_call | solution.py:237
  114.0 3.9 %back.4.refs_6_ = f32[56,384]{1,0:T(8,128)S(1)} custom-call(bf16[512,384]{1,0:T(8,128)(2,1)S(1)} %pad_maximum_fusion.i0.c0.refs_0_, bf16[512,384]{1,0:T(8,128)(2,1)S(1)} %collective-permute-done.16.i1.c1.refs_1_, f32[1024,384]{1,0:T(8,128)S(1)} %get-tuple-element.29.refs_2_, f32[1024,128]{1,0:T(8,128)S(1)} %get-tuple-element.30.refs_3_, ...), custom_call_target="tpu_custom_call" | custom-call | flops 1000000000 | bytes 16000000 | tf_op jit(solution)/shard_map/back/pallas_call | solution.py:320
  117.9 3.9 %back.5 = bf16[56,384]{1,0:T(8,128)(2,1)S(1)} custom-call(bf16[512,384]{1,0:T(8,128)(2,1)S(1)} %collective-permute-done.14.i2.c2.refs_0_, bf16[512,384]{1,0:T(8,128)(2,1)S(1)} %collective-permute-done.15.i3.c3.refs_1_, f32[1024,384]{1,0:T(8,128)S(1)} %get-tuple-element.29.refs_2_, f32[1024,128]{1,0:T(8,128)S(1)} %get-tuple-element.30.refs_3_, ...), custom_call_target="tpu_custom_call" | custom-call | flops 1000000000 | bytes 16000000 | tf_op jit(solution)/shard_map/back/pallas_call | solution.py:320
  121.8 1.3 collective-permute-start.20
  123.0 2.4 %collective-permute-start.21 = (bf16[56,384]{1,0:T(8,128)(2,1)S(1)}, bf16[56,384]{1,0:T(8,128)(2,1)S(1)}, u32[]{:S(2)}, u32[]{:S(2)}) collective-permute-start(bf16[56,384]{1,0:T(8,128)(2,1)S(1)} %back.5), channel_id=1, source_target_pairs={{0,2},{1,3},{2,0},{3,1},{4,6},{5,7},{6,4},{7,5},{8,10},{9,11},{10,... | collective-permute-start | bytes 129032 | tf_op jit(solution)/shard_map/ppermute | solution.py:42
  125.4 1.5 collective-permute-start.22
  129.9 1.6 collective-permute-start.25
  131.6 3.6 %collective-permute-start.24 = (f32[56,48]{1,0:T(8,128)S(1)}, f32[56,48]{1,0:T(8,128)S(1)}, u32[]{:S(2)}, u32[]{:S(2)}) collective-permute-start(f32[56,48]{1,0:T(8,128)S(1)} %fusion.27), channel_id=1, source_target_pairs={{240,0},{241,1},{242,2},{243,3},{244,4},{245,5},{246,6},{247,7},{2... | collective-permute-start | bytes 32264 | tf_op jit(solution)/shard_map/ppermute | solution.py:61
  135.2 2.8 %collective-permute-start.31 = (bf16[256,384]{1,0:T(8,128)(2,1)}, bf16[256,384]{1,0:T(8,128)(2,1)}, u32[]{:S(2)}, u32[]{:S(2)}) collective-permute-start(bf16[256,384]{1,0:T(8,128)(2,1)} %get-tuple-element.39), channel_id=1, source_target_pairs={{0,3},{1,0},{2,1},{3,2},{4,7},{5,4},{6,5},{7,6},{8,11},{9,8},{10,9... | collective-permute-start | bytes 589832 | tf_op jit(solution)/shard_map/ppermute | solution.py:42
  139.5 6.6 %collective-permute-done.26 = bf16[400,384]{1,0:T(8,128)(2,1)S(1)} collective-permute-done((bf16[400,384]{1,0:T(8,128)(2,1)}, bf16[400,384]{1,0:T(8,128)(2,1)S(1)}, u32[]{:S(2)}, u32[]{:S(2)}) %collective-permute-start.26) | collective-permute-done | bytes 307232 | tf_op jit(solution)/shard_map/ppermute | solution.py:47
  146.3 2.0 %collective-permute-start.27 = (bf16[400,384]{1,0:T(8,128)(2,1)S(1)}, bf16[400,384]{1,0:T(8,128)(2,1)S(1)}, u32[]{:S(2)}, u32[]{:S(2)}) collective-permute-start(bf16[400,384]{1,0:T(8,128)(2,1)S(1)} %get-tuple-element.68), channel_id=1, source_target_pairs={{240,0},{248,8},{0,16},{8,24},{16,32},{24,40},{32,48},{40,56},{48,... | collective-permute-start | bytes 921608 | tf_op jit(solution)/shard_map/ppermute | solution.py:66
  149.6 2.1 %add_convert_fusion = bf16[256,384]{1,0:T(8,128)(2,1)} fusion(bf16[256,384]{1,0:T(8,128)(2,1)} %collective-permute-done.33, bf16[256,384]{1,0:T(8,128)(2,1)} %collective-permute-done.32, bf16[256,384]{1,0:T(8,128)(2,1)} %collective-permute-done.31, bf16[256,384]{1,0:T(8,128)(2,1)} %get-tuple-element.38, f32[384]{0:T(512)S(1)} %get-tuple-element.67, ...), kind=kLoop, calls=%fused_computation.26 | loop fusion | flops 1179648 | bytes 1182720 | tf_op jit(solution)/shard_map/convert_element_type | solution.py:443
  151.6 5.2 %collective-permute-done.27 = bf16[400,384]{1,0:T(8,128)(2,1)S(1)} collective-permute-done((bf16[400,384]{1,0:T(8,128)(2,1)S(1)}, bf16[400,384]{1,0:T(8,128)(2,1)S(1)}, u32[]{:S(2)}, u32[]{:S(2)}) %collective-permute-start.27) | collective-permute-done | bytes 307232 | tf_op jit(solution)/shard_map/ppermute | solution.py:66
  157.7 2.5 %collective-permute-start.28 = (f32[48,384]{1,0:T(8,128)S(1)}, f32[48,384]{1,0:T(8,128)S(1)}, u32[]{:S(2)}, u32[]{:S(2)}) collective-permute-start(f32[48,384]{1,0:T(8,128)S(1)} %get-tuple-element.89), channel_id=1, source_target_pairs={{0,3},{1,0},{2,1},{3,2},{4,7},{5,4},{6,5},{7,6},{8,11},{9,8},{10,9... | collective-permute-start | bytes 221192 | tf_op jit(solution)/shard_map/ppermute | solution.py:42
  160.2 2.2 %collective-permute-start.29 = (f32[48,384]{1,0:T(8,128)S(1)}, f32[48,384]{1,0:T(8,128)S(1)}, u32[]{:S(2)}, u32[]{:S(2)}) collective-permute-start(f32[48,384]{1,0:T(8,128)S(1)} %get-tuple-element.88), channel_id=1, source_target_pairs={{0,2},{1,3},{2,0},{3,1},{4,6},{5,7},{6,4},{7,5},{8,10},{9,11},{10,... | collective-permute-start | bytes 221192 | tf_op jit(solution)/shard_map/ppermute | solution.py:42
  163.0 3.0 %collective-permute-done.29 = f32[48,384]{1,0:T(8,128)S(1)} collective-permute-done((f32[48,384]{1,0:T(8,128)S(1)}, f32[48,384]{1,0:T(8,128)S(1)}, u32[]{:S(2)}, u32[]{:S(2)}) %collective-permute-start.29) | collective-permute-done | bytes 73760 | tf_op jit(solution)/shard_map/ppermute | solution.py:42
  166.0 1.9 %collective-permute-done.30 = f32[48,384]{1,0:T(8,128)S(1)} collective-permute-done((f32[48,384]{1,0:T(8,128)S(1)}, f32[48,384]{1,0:T(8,128)S(1)}, u32[]{:S(2)}, u32[]{:S(2)}) %collective-permute-start.30) | collective-permute-done | bytes 73760 | tf_op jit(solution)/shard_map/ppermute | solution.py:42
  168.6 1.1 broadcast_in_dim_reshape.3
  (153 shorter events, 26.8 us)
Async XLA Ops:
  3.1 5.6 %collective-permute-start = (f32[54,96]{1,0:T(8,128)S(1)}, f32[54,96]{1,0:T(8,128)S(1)}, u32[]{:S(2)}, u32[]{:S(2)}) collective-permute-start(f32[54,96]{1,0:T(8,128)S(1)} %maximum_maximum_fusion), channel_id=1, source_target_pairs={{0,4},{1,5},{2,6},{3,7},{4,0},{5,1},{6,2},{7,3},{8,12},{9,13},{10,... | collective-permute-start | bytes 62216 | tf_op jit(solution)/shard_map/ppermute | solution.py:47
  8.5 8.6 %copy-start.24 = (f32[1,192]{1,0:T(1,128)S(1)}, f32[1,192]{1,0:T(1,128)}, u32[]{:S(2)}) copy-start(f32[1,192]{1,0:T(1,128)} %param.17) | copy-start | bytes 2308
  9.0 13.0 %collective-permute-start.1 = (bf16[408,384]{1,0:T(8,128)(2,1)S(1)}, bf16[408,384]{1,0:T(8,128)(2,1)S(1)}, u32[]{:S(2)}, u32[]{:S(2)}) collective-permute-start(bf16[408,384]{1,0:T(8,128)(2,1)S(1)} %get-tuple-element.100), channel_id=1, source_target_pairs={{0,3},{1,0},{2,1},{3,2},{4,7},{5,4},{6,5},{7,6},{8,11},{9,8},{10,9... | collective-permute-start | bytes 940040 | tf_op jit(solution)/shard_map/ppermute | solution.py:42
  10.9 26.1 %copy-start.13 = (f32[1,192,384]{2,1,0:T(8,128)S(1)}, f32[1,192,384]{2,1,0:T(8,128)}, u32[]{:S(2)}) copy-start(f32[1,192,384]{2,1,0:T(8,128)} %param.18) | copy-start | bytes 884740
  10.9 40.3 %collective-permute-start.5 = (bf16[256,384]{1,0:T(8,128)(2,1)}, bf16[256,384]{1,0:T(8,128)(2,1)}, u32[]{:S(2)}, u32[]{:S(2)}) collective-permute-start(bf16[256,384]{1,0:T(8,128)(2,1)} %bitcast.20.c0), channel_id=1, source_target_pairs={{0,1},{1,2},{2,3},{3,0},{4,5},{5,6},{6,7},{7,4},{8,9},{9,10},{10,1... | collective-permute-start | bytes 589832 | tf_op jit(solution)/shard_map/ppermute | solution.py:42
  11.9 39.3 %collective-permute-start.6 = (bf16[256,384]{1,0:T(8,128)(2,1)}, bf16[256,384]{1,0:T(8,128)(2,1)}, u32[]{:S(2)}, u32[]{:S(2)}) collective-permute-start(bf16[256,384]{1,0:T(8,128)(2,1)} %bitcast.20.c0), channel_id=1, source_target_pairs={{0,2},{1,3},{2,0},{3,1},{4,6},{5,7},{6,4},{7,5},{8,10},{9,11},{10,... | collective-permute-start | bytes 589832 | tf_op jit(solution)/shard_map/ppermute | solution.py:42
  13.2 38.0 %collective-permute-start.7 = (bf16[256,384]{1,0:T(8,128)(2,1)}, bf16[256,384]{1,0:T(8,128)(2,1)}, u32[]{:S(2)}, u32[]{:S(2)}) collective-permute-start(bf16[256,384]{1,0:T(8,128)(2,1)} %bitcast.20.c0), channel_id=1, source_target_pairs={{0,3},{1,0},{2,1},{3,2},{4,7},{5,4},{6,5},{7,6},{8,11},{9,8},{10,9... | collective-permute-start | bytes 589832 | tf_op jit(solution)/shard_map/ppermute | solution.py:42
  14.6 15.6 %collective-permute-start.2 = (bf16[408,384]{1,0:T(8,128)(2,1)S(1)}, bf16[408,384]{1,0:T(8,128)(2,1)S(1)}, u32[]{:S(2)}, u32[]{:S(2)}) collective-permute-start(bf16[408,384]{1,0:T(8,128)(2,1)S(1)} %get-tuple-element.99), channel_id=1, source_target_pairs={{0,2},{1,3},{2,0},{3,1},{4,6},{5,7},{6,4},{7,5},{8,10},{9,11},{10,... | collective-permute-start | bytes 940040 | tf_op jit(solution)/shard_map/ppermute | solution.py:42
  22.0 19.5 %copy-start = (bf16[408,384]{1,0:T(8,128)(2,1)}, bf16[408,384]{1,0:T(8,128)(2,1)S(1)}, u32[]{:S(2)}) copy-start(bf16[408,384]{1,0:T(8,128)(2,1)S(1)} %collective-permute-done.1.i3.refs_3_) | copy-start | bytes 940036
  22.0 14.1 %collective-permute-start.3 = (bf16[408,384]{1,0:T(8,128)(2,1)S(1)}, bf16[408,384]{1,0:T(8,128)(2,1)S(1)}, u32[]{:S(2)}, u32[]{:S(2)}) collective-permute-start(bf16[408,384]{1,0:T(8,128)(2,1)S(1)} %get-tuple-element.98), channel_id=1, source_target_pairs={{0,1},{1,2},{2,3},{3,0},{4,5},{5,6},{6,7},{7,4},{8,9},{9,10},{10,1... | collective-permute-start | bytes 940040 | tf_op jit(solution)/shard_map/ppermute | solution.py:42
  30.2 11.4 %copy-start.2 = (bf16[408,384]{1,0:T(8,128)(2,1)}, bf16[408,384]{1,0:T(8,128)(2,1)S(1)}, u32[]{:S(2)}) copy-start(bf16[408,384]{1,0:T(8,128)(2,1)S(1)} %collective-permute-done.2.i2.refs_2_) | copy-start | bytes 940036
  37.9 12.5 %collective-permute-start.4 = (bf16[400,384]{1,0:T(8,128)(2,1)}, bf16[400,384]{1,0:T(8,128)(2,1)}, u32[]{:S(2)}, u32[]{:S(2)}) collective-permute-start(bf16[400,384]{1,0:T(8,128)(2,1)} %fusion.2.own), channel_id=1, source_target_pairs={{0,4},{1,5},{2,6},{3,7},{4,0},{5,1},{6,2},{7,3},{8,12},{9,13},{10,... | collective-permute-start | bytes 921608 | tf_op jit(solution)/shard_map/ppermute | solution.py:47
  51.2 7.0 %copy-start.25 = (f32[1,192]{1,0:T(1,128)S(1)}, f32[1,192]{1,0:T(1,128)}, u32[]{:S(2)}) copy-start(f32[1,192]{1,0:T(1,128)} %param.22) | copy-start | bytes 2308
  57.8 15.4 %collective-permute-start.17 = (bf16[400,384]{1,0:T(8,128)(2,1)}, bf16[400,384]{1,0:T(8,128)(2,1)}, u32[]{:S(2)}, u32[]{:S(2)}) collective-permute-start(bf16[400,384]{1,0:T(8,128)(2,1)} %get-tuple-element.33), channel_id=1, source_target_pairs={{0,4},{1,5},{2,6},{3,7},{4,0},{5,1},{6,2},{7,3},{8,12},{9,13},{10,... | collective-permute-start | bytes 921608 | tf_op jit(solution)/shard_map/ppermute | solution.py:47
  63.3 9.9 %copy-start.7 = (f32[400,384]{1,0:T(8,128)S(1)}, f32[400,384]{1,0:T(8,128)}, u32[]{:S(2)}) copy-start(f32[400,384]{1,0:T(8,128)} %copy-done.6) | copy-start | bytes 1843204
  63.3 9.9 %copy-start.11 = (f32[4,48,384]{2,1,0:T(8,128)S(1)}, f32[4,48,384]{2,1,0:T(8,128)}, u32[]{:S(2)}) copy-start(f32[4,48,384]{2,1,0:T(8,128)} %copy-done.10) | copy-start | bytes 884740
  63.3 9.9 %copy-start.14 = (f32[1,192,384]{2,1,0:T(8,128)S(1)}, f32[1,192,384]{2,1,0:T(8,128)}, u32[]{:S(2)}) copy-start(f32[1,192,384]{2,1,0:T(8,128)} %param.18) | copy-start | bytes 884740
  63.3 9.9 %copy-start.20 = (f32[4,48,384]{2,1,0:T(8,128)S(1)}, f32[4,48,384]{2,1,0:T(8,128)}, u32[]{:S(2)}) copy-start(f32[4,48,384]{2,1,0:T(8,128)} %get-tuple-element.78) | copy-start | bytes 884740
  63.3 9.9 %copy-start.23 = (f32[1,192,384]{2,1,0:T(8,128)S(1)}, f32[1,192,384]{2,1,0:T(8,128)}, u32[]{:S(2)}) copy-start(f32[1,192,384]{2,1,0:T(8,128)} %param.23) | copy-start | bytes 884740
  70.9 4.4 %collective-permute-start.10 = (bf16[56,384]{1,0:T(8,128)(2,1)S(1)}, bf16[56,384]{1,0:T(8,128)(2,1)S(1)}, u32[]{:S(2)}, u32[]{:S(2)}) collective-permute-start(bf16[56,384]{1,0:T(8,128)(2,1)S(1)} %back.3), channel_id=1, source_target_pairs={{0,3},{1,0},{2,1},{3,2},{4,7},{5,4},{6,5},{7,6},{8,11},{9,8},{10,9... | collective-permute-start | bytes 129032 | tf_op jit(solution)/shard_map/ppermute | solution.py:42
  71.0 5.5 %collective-permute-start.8 = (bf16[56,384]{1,0:T(8,128)(2,1)S(1)}, bf16[56,384]{1,0:T(8,128)(2,1)S(1)}, u32[]{:S(2)}, u32[]{:S(2)}) collective-permute-start(bf16[56,384]{1,0:T(8,128)(2,1)S(1)} %back.3), channel_id=1, source_target_pairs={{0,1},{1,2},{2,3},{3,0},{4,5},{5,6},{6,7},{7,4},{8,9},{9,10},{10,1... | collective-permute-start | bytes 129032 | tf_op jit(solution)/shard_map/ppermute | solution.py:42
  73.0 5.5 %collective-permute-start.9 = (bf16[56,384]{1,0:T(8,128)(2,1)S(1)}, bf16[56,384]{1,0:T(8,128)(2,1)S(1)}, u32[]{:S(2)}, u32[]{:S(2)}) collective-permute-start(bf16[56,384]{1,0:T(8,128)(2,1)S(1)} %back.3), channel_id=1, source_target_pairs={{0,2},{1,3},{2,0},{3,1},{4,6},{5,7},{6,4},{7,5},{8,10},{9,11},{10,... | collective-permute-start | bytes 129032 | tf_op jit(solution)/shard_map/ppermute | solution.py:42
  73.3 13.6 %copy-start.12 = (f32[4,48,384]{2,1,0:T(8,128)S(1)}, f32[4,48,384]{2,1,0:T(8,128)}, u32[]{:S(2)}) copy-start(f32[4,48,384]{2,1,0:T(8,128)} %copy-done.10) | copy-start | bytes 884740
  73.3 13.6 %copy-start.15 = (f32[1,192,384]{2,1,0:T(8,128)S(1)}, f32[1,192,384]{2,1,0:T(8,128)}, u32[]{:S(2)}) copy-start(f32[1,192,384]{2,1,0:T(8,128)} %param.18) | copy-start | bytes 884740
  74.5 11.3 %collective-permute-start.18 = (bf16[400,384]{1,0:T(8,128)(2,1)S(1)}, bf16[400,384]{1,0:T(8,128)(2,1)}, u32[]{:S(2)}, u32[]{:S(2)}) collective-permute-start(bf16[400,384]{1,0:T(8,128)(2,1)S(1)} %get-tuple-element.72), channel_id=1, source_target_pairs={{248,0},{0,8},{8,16},{16,24},{24,32},{32,40},{40,48},{48,56},{56,6... | collective-permute-start | bytes 921608 | tf_op jit(solution)/shard_map/ppermute | solution.py:66
  78.6 4.7 %collective-permute-start.11 = (bf16[56,384]{1,0:T(8,128)(2,1)S(1)}, bf16[56,384]{1,0:T(8,128)(2,1)}, u32[]{:S(2)}, u32[]{:S(2)}) collective-permute-start(bf16[56,384]{1,0:T(8,128)(2,1)S(1)} %get-tuple-element.75), channel_id=1, source_target_pairs={{0,4},{1,5},{2,6},{3,7},{4,0},{5,1},{6,2},{7,3},{8,12},{9,13},{10,... | collective-permute-start | bytes 129032 | tf_op jit(solution)/shard_map/ppermute | solution.py:47
  80.3 14.0 %collective-permute-start.14 = (bf16[512,384]{1,0:T(8,128)(2,1)S(1)}, bf16[512,384]{1,0:T(8,128)(2,1)S(1)}, u32[]{:S(2)}, u32[]{:S(2)}) collective-permute-start(bf16[512,384]{1,0:T(8,128)(2,1)S(1)} %pad_maximum_fusion.i0.c0.refs_0_), channel_id=1, source_target_pairs={{0,2},{1,3},{2,0},{3,1},{4,6},{5,7},{6,4},{7,5},{8,10},{9,11},{10,... | collective-permute-start | bytes 1179656 | tf_op jit(solution)/shard_map/ppermute | solution.py:42
  81.0 19.0 %collective-permute-start.15 = (bf16[512,384]{1,0:T(8,128)(2,1)S(1)}, bf16[512,384]{1,0:T(8,128)(2,1)S(1)}, u32[]{:S(2)}, u32[]{:S(2)}) collective-permute-start(bf16[512,384]{1,0:T(8,128)(2,1)S(1)} %pad_maximum_fusion.i0.c0.refs_0_), channel_id=1, source_target_pairs={{0,3},{1,0},{2,1},{3,2},{4,7},{5,4},{6,5},{7,6},{8,11},{9,8},{10,9... | collective-permute-start | bytes 1179656 | tf_op jit(solution)/shard_map/ppermute | solution.py:42
  83.0 17.5 %collective-permute-start.16 = (bf16[512,384]{1,0:T(8,128)(2,1)S(1)}, bf16[512,384]{1,0:T(8,128)(2,1)S(1)}, u32[]{:S(2)}, u32[]{:S(2)}) collective-permute-start(bf16[512,384]{1,0:T(8,128)(2,1)S(1)} %pad_maximum_fusion.i0.c0.refs_0_), channel_id=1, source_target_pairs={{0,1},{1,2},{2,3},{3,0},{4,5},{5,6},{6,7},{7,4},{8,9},{9,10},{10,1... | collective-permute-start | bytes 1179656 | tf_op jit(solution)/shard_map/ppermute | solution.py:42
  83.3 8.3 %collective-permute-start.13 = (bf16[56,384]{1,0:T(8,128)(2,1)S(1)}, bf16[56,384]{1,0:T(8,128)(2,1)S(1)}, u32[]{:S(2)}, u32[]{:S(2)}) collective-permute-start(bf16[56,384]{1,0:T(8,128)(2,1)S(1)} %get-tuple-element.75), channel_id=1, source_target_pairs={{252,0},{253,1},{254,2},{255,3},{248,4},{249,5},{250,6},{251,7},{4... | collective-permute-start | bytes 129032 | tf_op jit(solution)/shard_map/ppermute | solution.py:61
  85.8 7.6 %collective-permute-start.12 = (f32[56,384]{1,0:T(8,128)S(1)}, f32[56,384]{1,0:T(8,128)S(1)}, u32[]{:S(2)}, u32[]{:S(2)}) collective-permute-start(f32[56,384]{1,0:T(8,128)S(1)} %get-tuple-element.74), channel_id=1, source_target_pairs={{248,0},{249,1},{250,2},{251,3},{252,4},{253,5},{254,6},{255,7},{0... | collective-permute-start | bytes 258056 | tf_op jit(solution)/shard_map/ppermute | solution.py:61
  88.0 20.6 %copy-start.16 = (f32[400,384]{1,0:T(8,128)}, f32[400,384]{1,0:T(8,128)S(1)}, u32[]{:S(2)}) copy-start(f32[400,384]{1,0:T(8,128)S(1)} %get-tuple-element.71) | copy-start | bytes 1843204
  91.6 17.1 %collective-permute-start.19 = (bf16[400,384]{1,0:T(8,128)(2,1)S(1)}, bf16[400,384]{1,0:T(8,128)(2,1)S(1)}, u32[]{:S(2)}, u32[]{:S(2)}) collective-permute-start(bf16[400,384]{1,0:T(8,128)(2,1)S(1)} %get-tuple-element.70.own), channel_id=1, source_target_pairs={{0,4},{1,5},{2,6},{3,7},{4,0},{5,1},{6,2},{7,3},{8,12},{9,13},{10,... | collective-permute-start | bytes 921608 | tf_op jit(solution)/shard_map/ppermute | solution.py:47
  117.9 28.2 %copy-start.17 = (f32[400,384]{1,0:T(8,128)S(1)}, f32[400,384]{1,0:T(8,128)}, u32[]{:S(2)}) copy-start(f32[400,384]{1,0:T(8,128)} %copy-done.16) | copy-start | bytes 1843204
  121.8 6.0 %collective-permute-start.20 = (bf16[56,384]{1,0:T(8,128)(2,1)S(1)}, bf16[56,384]{1,0:T(8,128)(2,1)S(1)}, u32[]{:S(2)}, u32[]{:S(2)}) collective-permute-start(bf16[56,384]{1,0:T(8,128)(2,1)S(1)} %back.5), channel_id=1, source_target_pairs={{0,1},{1,2},{2,3},{3,0},{4,5},{5,6},{6,7},{7,4},{8,9},{9,10},{10,1... | collective-permute-start | bytes 129032 | tf_op jit(solution)/shard_map/ppermute | solution.py:42
  123.0 5.5 %collective-permute-start.21 = (bf16[56,384]{1,0:T(8,128)(2,1)S(1)}, bf16[56,384]{1,0:T(8,128)(2,1)S(1)}, u32[]{:S(2)}, u32[]{:S(2)}) collective-permute-start(bf16[56,384]{1,0:T(8,128)(2,1)S(1)} %back.5), channel_id=1, source_target_pairs={{0,2},{1,3},{2,0},{3,1},{4,6},{5,7},{6,4},{7,5},{8,10},{9,11},{10,... | collective-permute-start | bytes 129032 | tf_op jit(solution)/shard_map/ppermute | solution.py:42
  125.4 4.0 %collective-permute-start.22 = (bf16[56,384]{1,0:T(8,128)(2,1)S(1)}, bf16[56,384]{1,0:T(8,128)(2,1)S(1)}, u32[]{:S(2)}, u32[]{:S(2)}) collective-permute-start(bf16[56,384]{1,0:T(8,128)(2,1)S(1)} %back.5), channel_id=1, source_target_pairs={{0,3},{1,0},{2,1},{3,2},{4,7},{5,4},{6,5},{7,6},{8,11},{9,8},{10,9... | collective-permute-start | bytes 129032 | tf_op jit(solution)/shard_map/ppermute | solution.py:42
  129.6 8.6 %collective-permute-start.23 = (bf16[56,48]{1,0:T(8,128)(2,1)S(1)}, bf16[56,48]{1,0:T(8,128)(2,1)S(1)}, u32[]{:S(2)}, u32[]{:S(2)}) collective-permute-start(bf16[56,48]{1,0:T(8,128)(2,1)S(1)} %constant_dynamic-slice_fusion.5), channel_id=1, source_target_pairs={{0,4},{1,5},{2,6},{3,7},{4,0},{5,1},{6,2},{7,3},{8,12},{9,13},{10,... | collective-permute-start | bytes 16136 | tf_op jit(solution)/shard_map/ppermute | solution.py:47
  129.9 9.1 %collective-permute-start.25 = (bf16[56,48]{1,0:T(8,128)(2,1)S(1)}, bf16[56,48]{1,0:T(8,128)(2,1)S(1)}, u32[]{:S(2)}, u32[]{:S(2)}) collective-permute-start(bf16[56,48]{1,0:T(8,128)(2,1)S(1)} %constant_dynamic-slice_fusion.5), channel_id=1, source_target_pairs={{244,0},{245,1},{246,2},{247,3},{240,4},{241,5},{242,6},{243,7},{2... | collective-permute-start | bytes 16136 | tf_op jit(solution)/shard_map/ppermute | solution.py:61
  131.6 7.7 %collective-permute-start.24 = (f32[56,48]{1,0:T(8,128)S(1)}, f32[56,48]{1,0:T(8,128)S(1)}, u32[]{:S(2)}, u32[]{:S(2)}) collective-permute-start(f32[56,48]{1,0:T(8,128)S(1)} %fusion.27), channel_id=1, source_target_pairs={{240,0},{241,1},{242,2},{243,3},{244,4},{245,5},{246,6},{247,7},{2... | collective-permute-start | bytes 32264 | tf_op jit(solution)/shard_map/ppermute | solution.py:61
  135.2 14.3 %collective-permute-start.31 = (bf16[256,384]{1,0:T(8,128)(2,1)}, bf16[256,384]{1,0:T(8,128)(2,1)}, u32[]{:S(2)}, u32[]{:S(2)}) collective-permute-start(bf16[256,384]{1,0:T(8,128)(2,1)} %get-tuple-element.39), channel_id=1, source_target_pairs={{0,3},{1,0},{2,1},{3,2},{4,7},{5,4},{6,5},{7,6},{8,11},{9,8},{10,9... | collective-permute-start | bytes 589832 | tf_op jit(solution)/shard_map/ppermute | solution.py:42
  138.0 11.5 %collective-permute-start.32 = (bf16[256,384]{1,0:T(8,128)(2,1)}, bf16[256,384]{1,0:T(8,128)(2,1)}, u32[]{:S(2)}, u32[]{:S(2)}) collective-permute-start(bf16[256,384]{1,0:T(8,128)(2,1)} %get-tuple-element.40), channel_id=1, source_target_pairs={{0,2},{1,3},{2,0},{3,1},{4,6},{5,7},{6,4},{7,5},{8,10},{9,11},{10,... | collective-permute-start | bytes 589832 | tf_op jit(solution)/shard_map/ppermute | solution.py:42
  138.2 11.4 %collective-permute-start.33 = (bf16[256,384]{1,0:T(8,128)(2,1)}, bf16[256,384]{1,0:T(8,128)(2,1)}, u32[]{:S(2)}, u32[]{:S(2)}) collective-permute-start(bf16[256,384]{1,0:T(8,128)(2,1)} %get-tuple-element.41), channel_id=1, source_target_pairs={{0,1},{1,2},{2,3},{3,0},{4,5},{5,6},{6,7},{7,4},{8,9},{9,10},{10,1... | collective-permute-start | bytes 589832 | tf_op jit(solution)/shard_map/ppermute | solution.py:42
  139.0 7.1 %collective-permute-start.26 = (bf16[400,384]{1,0:T(8,128)(2,1)}, bf16[400,384]{1,0:T(8,128)(2,1)S(1)}, u32[]{:S(2)}, u32[]{:S(2)}) collective-permute-start(bf16[400,384]{1,0:T(8,128)(2,1)} %get-tuple-element.37), channel_id=1, source_target_pairs={{0,4},{1,5},{2,6},{3,7},{4,0},{5,1},{6,2},{7,3},{8,12},{9,13},{10,... | collective-permute-start | bytes 921608 | tf_op jit(solution)/shard_map/ppermute | solution.py:47
  146.3 10.5 %collective-permute-start.27 = (bf16[400,384]{1,0:T(8,128)(2,1)S(1)}, bf16[400,384]{1,0:T(8,128)(2,1)S(1)}, u32[]{:S(2)}, u32[]{:S(2)}) collective-permute-start(bf16[400,384]{1,0:T(8,128)(2,1)S(1)} %get-tuple-element.68), channel_id=1, source_target_pairs={{240,0},{248,8},{0,16},{8,24},{16,32},{24,40},{32,48},{40,56},{48,... | collective-permute-start | bytes 921608 | tf_op jit(solution)/shard_map/ppermute | solution.py:66
  157.7 5.3 %collective-permute-start.28 = (f32[48,384]{1,0:T(8,128)S(1)}, f32[48,384]{1,0:T(8,128)S(1)}, u32[]{:S(2)}, u32[]{:S(2)}) collective-permute-start(f32[48,384]{1,0:T(8,128)S(1)} %get-tuple-element.89), channel_id=1, source_target_pairs={{0,3},{1,0},{2,1},{3,2},{4,7},{5,4},{6,5},{7,6},{8,11},{9,8},{10,9... | collective-permute-start | bytes 221192 | tf_op jit(solution)/shard_map/ppermute | solution.py:42
  160.2 5.9 %collective-permute-start.29 = (f32[48,384]{1,0:T(8,128)S(1)}, f32[48,384]{1,0:T(8,128)S(1)}, u32[]{:S(2)}, u32[]{:S(2)}) collective-permute-start(f32[48,384]{1,0:T(8,128)S(1)} %get-tuple-element.88), channel_id=1, source_target_pairs={{0,2},{1,3},{2,0},{3,1},{4,6},{5,7},{6,4},{7,5},{8,10},{9,11},{10,... | collective-permute-start | bytes 221192 | tf_op jit(solution)/shard_map/ppermute | solution.py:42
  162.4 5.6 %collective-permute-start.30 = (f32[48,384]{1,0:T(8,128)S(1)}, f32[48,384]{1,0:T(8,128)S(1)}, u32[]{:S(2)}, u32[]{:S(2)}) collective-permute-start(f32[48,384]{1,0:T(8,128)S(1)} %get-tuple-element.87), channel_id=1, source_target_pairs={{0,1},{1,2},{2,3},{3,0},{4,5},{5,6},{6,7},{7,4},{8,9},{9,10},{10,1... | collective-permute-start | bytes 221192 | tf_op jit(solution)/shard_map/ppermute | solution.py:42
  (12 other events, 33.8 us)
where the time goes:
time: 171 us; the launch traced here: 170 us
  waiting for transfers between devices  52.9 us (31%)
  starting transfers between devices  43.6 us (25%)
  Pallas kernels  42.6 us (25%)
  local copies, waits for them, and re-layouts  18.6 us (11%)
  other arithmetic  10.8 us (6%)
    ppermute x21, waiting for transfers between devices, shift(): return lax.ppermute(block, 'grp', route)  35.6 us
    ppermute x21, starting transfers between devices, shift(): return lax.ppermute(block, 'grp', route)  25.9 us
    pallas_call x2, Pallas kernels, front(): pl.pallas_call(front_kernel, out_shape=(jax.ShapeDtypeStruct((total, CHAN...  16.2 us
    pallas_call x3, Pallas kernels, back(): pl.pallas_call(functools.partial(back_kernel, start, count, final), out_s...  15.3 us
    pallas_call x2, Pallas kernels, mlp(): pl.pallas_call(functools.partial(mlp_kernel, last), out_shape=tuple(shape...  11.1 us
    unnamed x74, local copies, waits for them, and re-layouts  9.55 us
    ppermute x7, starting transfers between devices, swap(): return lax.ppermute(block, 'grp', route)  8.05 us
    ppermute x4, starting transfers between devices, pair_along(): return lax.ppermute(block, ('peer', 'grp'), route)  7.59 us
  transfers between devices with their start and end apart: 34, of which 18 were waited for; matrix products, arithmetic and copies ran while one was open for 11% of the time, Pallas kernels for 14%

commit v1 on v0

--- a/solution.py
+++ b/solution.py
@@ -421,8 +421,6 @@
     for step in range(STEPS):
         last = step == STEPS - 1
         base = small - (RATE * MOMENTUM) * small_m
-        if last:
-            base = columns_of(base, member)
         own = weights.astype(BF16)
         other = swap(own)
         normed, scaled, spread = front(step_images[step], small)
@@ -447,17 +445,16 @@
         weights = 0.5 * (weights + theirs.astype(F32))
         rest = [shift(d_small, k) for k in range(1, RING)]
         half_sum = d_small.astype(F32) + sum(r.astype(F32) for r in rest)
-        mine = theirs = half_sum.astype(BF16)
-        if last:
-            mine, theirs = columns_of(mine, member), columns_of(theirs, (1 - y) * RING + x)
-        near = swap(theirs).astype(F32)
+        mine = half_sum.astype(BF16)
+        near = swap(mine).astype(F32)
         part_step = base - RATE * mine.astype(F32)
         far_own = pair_along(part_step, 2**step, False)
-        far_pair = pair_along(theirs, 2**step, True).astype(F32)
+        far_pair = pair_along(mine, 2**step, True).astype(F32)
         grad = mine.astype(F32) + near
         small = 0.5 * ((base - RATE * grad) + (far_own - RATE * far_pair))
         small_m = MOMENTUM * small_m + grad if not last else None
 
+    small = columns_of(small, member)
     new_bin = lax.dynamic_slice_in_dim(weights[2 * BLOCK], y * BLOCK, BLOCK, 0)
     share = weights[BLOCK : 2 * BLOCK]
 

time: 171 us -> 171 us (level)
  waiting for transfers between devices: 52.9 us -> 55.5 us
  other arithmetic: 10.8 us -> 8.73 us
    unnamed x74 -> x71, local copies, waits for them, and re-layouts: 9.55 us -> 9.46 us
  transfers between devices with their start and end apart: 34 -> 34, of which waited for: 18 -> 21; matrix products, arithmetic and copies ran while one was open for 11% -> 9% of each run, Pallas kernels for 14% -> 14%
where the time goes in v1:
time: 171 us; the launch traced here: 169 us
  waiting for transfers between devices  55.5 us (32%)
  starting transfers between devices  43.8 us (26%)
  Pallas kernels  42.5 us (25%)
  local copies, waits for them, and re-layouts  17.8 us (10%)
  other arithmetic  8.73 us (5%)
    ppermute x21, waiting for transfers between devices, shift(): return lax.ppermute(block, 'grp', route)  37.3 us
    ppermute x21, starting transfers between devices, shift(): return lax.ppermute(block, 'grp', route)  25.9 us
    pallas_call x2, Pallas kernels, front(): pl.pallas_call(front_kernel, out_shape=(jax.ShapeDtypeStruct((total, CHAN...  16.2 us
    pallas_call x3, Pallas kernels, back(): pl.pallas_call(functools.partial(back_kernel, start, count, final), out_s...  15.3 us
    pallas_call x2, Pallas kernels, mlp(): pl.pallas_call(functools.partial(mlp_kernel, last), out_shape=tuple(shape...  11.1 us
    unnamed x71, local copies, waits for them, and re-layouts  9.46 us
    ppermute x7, starting transfers between devices, swap(): return lax.ppermute(block, 'grp', route)  8.29 us
    ppermute x4, starting transfers between devices, pair_along(): return lax.ppermute(block, ('peer', 'grp'), route)  7.49 us
  transfers between devices with their start and end apart: 34, of which 21 were waited for; matrix products, arithmetic and copies ran while one was open for 9% of the time, Pallas kernels for 14%

profile of v1, /device:TPU:8, one launch (start us, length us, event | category | flops | bytes accessed | tf_op | source)
XLA Modules:
  0.0 169.5 jit_solution(1975346127903577146)
XLA Ops:
  3.1 2.2 %collective-permute-start = (f32[54,96]{1,0:T(8,128)S(1)}, f32[54,96]{1,0:T(8,128)S(1)}, u32[]{:S(2)}, u32[]{:S(2)}) collective-permute-start(f32[54,96]{1,0:T(8,128)S(1)} %maximum_maximum_fusion), channel_id=1, source_target_pairs={{0,4},{1,5},{2,6},{3,7},{4,0},{5,1},{6,2},{7,3},{8,12},{9,13},{10,... | collective-permute-start | bytes 62216 | tf_op jit(solution)/shard_map/ppermute | solution.py:47
  5.3 1.7 %fusion.35 = (bf16[1,1,1,8,32,384]{5,4,3,2,1,0:T(8,128)(2,1)S(1)}, bf16[1,1,1,8,32,384]{5,4,3,2,1,0:T(8,128)(2,1)}) fusion(bf16[2,1,1,8,32,384]{5,4,3,2,1,0:T(8,128)(2,1)} %param.12), kind=kLoop, calls=%fused_computation.128 | loop fusion | bytes 786432 | tf_op jit(solution)/shard_map/slice | solution.py:357
  7.0 1.1 convert_bitcast_fusion
  9.0 1.1 collective-permute-start.1
  11.9 1.3 collective-permute-start.6
  13.2 1.4 collective-permute-start.7
  14.6 2.5 %collective-permute-start.2 = (bf16[408,384]{1,0:T(8,128)(2,1)S(1)}, bf16[408,384]{1,0:T(8,128)(2,1)S(1)}, u32[]{:S(2)}, u32[]{:S(2)}) collective-permute-start(bf16[408,384]{1,0:T(8,128)(2,1)S(1)} %get-tuple-element.103), channel_id=1, source_target_pairs={{0,2},{1,3},{2,0},{3,1},{4,6},{5,7},{6,4},{7,5},{8,10},{9,11},{10,... | collective-permute-start | bytes 940040 | tf_op jit(solution)/shard_map/ppermute | solution.py:42
  17.2 4.8 %collective-permute-done.1.i3.refs_3_ = bf16[408,384]{1,0:T(8,128)(2,1)S(1)} collective-permute-done((bf16[408,384]{1,0:T(8,128)(2,1)S(1)}, bf16[408,384]{1,0:T(8,128)(2,1)S(1)}, u32[]{:S(2)}, u32[]{:S(2)}) %collective-permute-start.1) | collective-permute-done | bytes 313376 | tf_op jit(solution)/shard_map/ppermute | solution.py:42
  22.0 8.1 %collective-permute-done.2.i2.refs_2_ = bf16[408,384]{1,0:T(8,128)(2,1)S(1)} collective-permute-done((bf16[408,384]{1,0:T(8,128)(2,1)S(1)}, bf16[408,384]{1,0:T(8,128)(2,1)S(1)}, u32[]{:S(2)}, u32[]{:S(2)}) %collective-permute-start.2) | collective-permute-done | bytes 313376 | tf_op jit(solution)/shard_map/ppermute | solution.py:42
  30.2 5.9 %collective-permute-done.3.i1.refs_1_ = bf16[408,384]{1,0:T(8,128)(2,1)S(1)} collective-permute-done((bf16[408,384]{1,0:T(8,128)(2,1)S(1)}, bf16[408,384]{1,0:T(8,128)(2,1)S(1)}, u32[]{:S(2)}, u32[]{:S(2)}) %collective-permute-start.3) | collective-permute-done | bytes 313376 | tf_op jit(solution)/shard_map/ppermute | solution.py:42
  37.9 1.6 collective-permute-start.4
  41.5 8.1 %front.2 = (bf16[1024,384]{1,0:T(8,128)(2,1)S(1)}, f32[1024,384]{1,0:T(8,128)S(1)}, f32[1024,128]{1,0:T(8,128)S(1)}) custom-call(bf16[256,384]{1,0:T(8,128)(2,1)S(1)} %bitcast.86, bf16[408,384]{1,0:T(8,128)(2,1)S(1)} %collective-permute-done.3.i1.refs_1_, bf16[408,384]{1,0:T(8,128)(2,1)S(1)} %collective-permute-done.2.i2.refs_2_, ...), custom_call_target="tpu_custom_call" | custom-call | flops 1000000000 | bytes 30000000 | tf_op jit(solution)/shard_map/front/pallas_call | solution.py:135
  51.3 5.7 %mlp.2 = (f32[400,384]{1,0:T(8,128)S(1)}, bf16[400,384]{1,0:T(8,128)(2,1)}, f32[1024,384]{1,0:T(8,128)S(1)}, f32[8,384]{1,0:T(8,128)S(1)}) custom-call(s32[1]{0:T(128)} %bitcast.13.y_ref, bf16[1024,384]{1,0:T(8,128)(2,1)S(1)} %get-tuple-element.26.normed, bf16[400,384]{1,0:T(8,128)(2,1)} %fusion.2.own, bf16[400,384]{1,0:T(8,128)(2,1)} %collective-permute-done.4.other, ...), custom_call_target="tpu_custom_call" | custom-call | flops 2000000000 | bytes 20000000 | tf_op jit(solution)/shard_map/mlp/pallas_call | solution.py:237
  58.3 1.0 copy.48
  62.3 1.0 copy-done.9
  63.4 7.5 %back.3 = bf16[56,384]{1,0:T(8,128)(2,1)S(1)} custom-call(bf16[256,384]{1,0:T(8,128)(2,1)S(1)} %bitcast.87, bf16[408,384]{1,0:T(8,128)(2,1)S(1)} %copy-done.5, bf16[408,384]{1,0:T(8,128)(2,1)S(1)} %copy-done.3, bf16[408,384]{1,0:T(8,128)(2,1)S(1)} %copy-done.1, f32[1024,384]{1,0:T(8,128)S(1)} %get-tuple-element.24.refs_4_, f32[1024,128]{1,0:T(8,128)S(1)} %copy-done.9, ...), custom_call_target="tpu_custom_call" | custom-call | flops 1000000000 | bytes 32000000 | tf_op jit(solution)/shard_map/back/pallas_call | solution.py:320
  71.0 2.0 %collective-permute-start.8 = (bf16[56,384]{1,0:T(8,128)(2,1)S(1)}, bf16[56,384]{1,0:T(8,128)(2,1)S(1)}, u32[]{:S(2)}, u32[]{:S(2)}) collective-permute-start(bf16[56,384]{1,0:T(8,128)(2,1)S(1)} %back.3), channel_id=1, source_target_pairs={{0,1},{1,2},{2,3},{3,0},{4,5},{5,6},{6,7},{7,4},{8,9},{9,10},{10,1... | collective-permute-start | bytes 129032 | tf_op jit(solution)/shard_map/ppermute | solution.py:42
  73.3 1.2 fusion.28
  75.3 1.2 collective-permute-done.8
  76.5 2.0 %collective-permute-done.9 = bf16[56,384]{1,0:T(8,128)(2,1)S(1)} collective-permute-done((bf16[56,384]{1,0:T(8,128)(2,1)S(1)}, bf16[56,384]{1,0:T(8,128)(2,1)S(1)}, u32[]{:S(2)}, u32[]{:S(2)}) %collective-permute-start.9) | collective-permute-done | bytes 43040 | tf_op jit(solution)/shard_map/ppermute | solution.py:42
  78.6 1.7 collective-permute-start.11
  81.0 2.1 %collective-permute-start.15 = (bf16[512,384]{1,0:T(8,128)(2,1)S(1)}, bf16[512,384]{1,0:T(8,128)(2,1)S(1)}, u32[]{:S(2)}, u32[]{:S(2)}) collective-permute-start(bf16[512,384]{1,0:T(8,128)(2,1)S(1)} %pad_maximum_fusion.i0.c0.refs_0_), channel_id=1, source_target_pairs={{0,3},{1,0},{2,1},{3,2},{4,7},{5,4},{6,5},{7,6},{8,11},{9,8},{10,9... | collective-permute-start | bytes 1179656 | tf_op jit(solution)/shard_map/ppermute | solution.py:42
  83.2 1.2 collective-permute-start.13
  84.4 1.3 collective-permute-done.18
  85.6 1.0 collective-permute-start.12
  86.8 4.5 %collective-permute-done.13 = bf16[56,384]{1,0:T(8,128)(2,1)S(1)} collective-permute-done((bf16[56,384]{1,0:T(8,128)(2,1)S(1)}, bf16[56,384]{1,0:T(8,128)(2,1)S(1)}, u32[]{:S(2)}, u32[]{:S(2)}) %collective-permute-start.13) | collective-permute-done | bytes 43040 | tf_op jit(solution)/shard_map/ppermute | solution.py:61
  91.3 1.6 collective-permute-start.19
  93.9 6.0 %collective-permute-done.15.i3.c3.refs_1_ = bf16[512,384]{1,0:T(8,128)(2,1)S(1)} collective-permute-done((bf16[512,384]{1,0:T(8,128)(2,1)S(1)}, bf16[512,384]{1,0:T(8,128)(2,1)S(1)}, u32[]{:S(2)}, u32[]{:S(2)}) %collective-permute-start.15) | collective-permute-done | bytes 393248 | tf_op jit(solution)/shard_map/ppermute | solution.py:42
  100.4 8.1 %front.3 = (bf16[1024,384]{1,0:T(8,128)(2,1)S(1)}, f32[1024,384]{1,0:T(8,128)S(1)}, f32[1024,128]{1,0:T(8,128)S(1)}) custom-call(bf16[512,384]{1,0:T(8,128)(2,1)S(1)} %pad_maximum_fusion.i0.c0.refs_0_, bf16[512,384]{1,0:T(8,128)(2,1)S(1)} %collective-permute-done.16.i1.c1.refs_1_, bf16[512,384]{1,0:T(8,128)(2,1)S(1)} %collective-permute-done.14.i2.c2.refs_0_, ...), custom_call_target="tpu_custom_call" | custom-call | flops 1000000000 | bytes 30000000 | tf_op jit(solution)/shard_map/front/pallas_call | solution.py:135
  108.6 5.4 %mlp.3 = (f32[400,384]{1,0:T(8,128)S(1)}, bf16[400,384]{1,0:T(8,128)(2,1)}, f32[1024,384]{1,0:T(8,128)S(1)}, f32[8,384]{1,0:T(8,128)S(1)}, bf16[256,384]{1,0:T(8...) custom-call(s32[1]{0:T(128)} %bitcast.13.y_ref, ...), custom_call_target="tpu_custom_call" | custom-call | flops 2000000000 | bytes 20000000 | tf_op jit(solution)/shard_map/mlp/pallas_call | solution.py:237
  113.9 3.9 %back.4.refs_6_ = f32[56,384]{1,0:T(8,128)S(1)} custom-call(bf16[512,384]{1,0:T(8,128)(2,1)S(1)} %pad_maximum_fusion.i0.c0.refs_0_, bf16[512,384]{1,0:T(8,128)(2,1)S(1)} %collective-permute-done.16.i1.c1.refs_1_, f32[1024,384]{1,0:T(8,128)S(1)} %get-tuple-element.29.refs_2_, f32[1024,128]{1,0:T(8,128)S(1)} %get-tuple-element.30.refs_3_, ...), custom_call_target="tpu_custom_call" | custom-call | flops 1000000000 | bytes 16000000 | tf_op jit(solution)/shard_map/back/pallas_call | solution.py:320
  117.8 3.9 %back.5 = bf16[56,384]{1,0:T(8,128)(2,1)S(1)} custom-call(bf16[512,384]{1,0:T(8,128)(2,1)S(1)} %collective-permute-done.14.i2.c2.refs_0_, bf16[512,384]{1,0:T(8,128)(2,1)S(1)} %collective-permute-done.15.i3.c3.refs_1_, f32[1024,384]{1,0:T(8,128)S(1)} %get-tuple-element.29.refs_2_, f32[1024,128]{1,0:T(8,128)S(1)} %get-tuple-element.30.refs_3_, ...), custom_call_target="tpu_custom_call" | custom-call | flops 1000000000 | bytes 16000000 | tf_op jit(solution)/shard_map/back/pallas_call | solution.py:320
  121.7 1.3 collective-permute-start.20
  123.0 2.4 %collective-permute-start.21 = (bf16[56,384]{1,0:T(8,128)(2,1)S(1)}, bf16[56,384]{1,0:T(8,128)(2,1)S(1)}, u32[]{:S(2)}, u32[]{:S(2)}) collective-permute-start(bf16[56,384]{1,0:T(8,128)(2,1)S(1)} %back.5), channel_id=1, source_target_pairs={{0,2},{1,3},{2,0},{3,1},{4,6},{5,7},{6,4},{7,5},{8,10},{9,11},{10,... | collective-permute-start | bytes 129032 | tf_op jit(solution)/shard_map/ppermute | solution.py:42
  125.4 1.5 collective-permute-start.22
  127.5 1.0 collective-permute-done.21
  129.8 1.6 collective-permute-start.25
  131.5 3.6 %collective-permute-start.24 = (f32[56,384]{1,0:T(8,128)S(1)}, f32[56,384]{1,0:T(8,128)S(1)}, u32[]{:S(2)}, u32[]{:S(2)}) collective-permute-start(f32[56,384]{1,0:T(8,128)S(1)} %get-tuple-element.72), channel_id=1, source_target_pairs={{240,0},{241,1},{242,2},{243,3},{244,4},{245,5},{246,6},{247,7},{2... | collective-permute-start | bytes 258056 | tf_op jit(solution)/shard_map/ppermute | solution.py:61
  135.1 2.8 %collective-permute-start.31 = (bf16[256,384]{1,0:T(8,128)(2,1)}, bf16[256,384]{1,0:T(8,128)(2,1)S(1)}, u32[]{:S(2)}, u32[]{:S(2)}) collective-permute-start(bf16[256,384]{1,0:T(8,128)(2,1)} %get-tuple-element.39), channel_id=1, source_target_pairs={{0,3},{1,0},{2,1},{3,2},{4,7},{5,4},{6,5},{7,6},{8,11},{9,8},{10,9... | collective-permute-start | bytes 589832 | tf_op jit(solution)/shard_map/ppermute | solution.py:42
  139.8 6.1 %collective-permute-done.26 = bf16[400,384]{1,0:T(8,128)(2,1)S(1)} collective-permute-done((bf16[400,384]{1,0:T(8,128)(2,1)}, bf16[400,384]{1,0:T(8,128)(2,1)S(1)}, u32[]{:S(2)}, u32[]{:S(2)}) %collective-permute-start.26) | collective-permute-done | bytes 307232 | tf_op jit(solution)/shard_map/ppermute | solution.py:47
  146.1 2.0 %collective-permute-start.27 = (bf16[400,384]{1,0:T(8,128)(2,1)S(1)}, bf16[400,384]{1,0:T(8,128)(2,1)S(1)}, u32[]{:S(2)}, u32[]{:S(2)}) collective-permute-start(bf16[400,384]{1,0:T(8,128)(2,1)S(1)} %get-tuple-element.68), channel_id=1, source_target_pairs={{240,0},{248,8},{0,16},{8,24},{16,32},{24,40},{32,48},{40,56},{48,... | collective-permute-start | bytes 921608 | tf_op jit(solution)/shard_map/ppermute | solution.py:66
  149.4 1.9 %add_convert_fusion = bf16[256,384]{1,0:T(8,128)(2,1)} fusion(bf16[256,384]{1,0:T(8,128)(2,1)} %collective-permute-done.33, bf16[256,384]{1,0:T(8,128)(2,1)} %collective-permute-done.32, bf16[256,384]{1,0:T(8,128)(2,1)S(1)} %collective-permute-done.31, bf16[256,384]{1,0:T(8,128)(2,1)S(1)} %copy-done.22, f32[384]{0:T(512)S(1)} %get-tuple-element.67, ...), kind=kLoop, calls=%fused_computation.26 | loop fusion | flops 1179648 | bytes 1182720 | tf_op jit(solution)/shard_map/convert_element_type | solution.py:441
  151.2 5.4 %collective-permute-done.27 = bf16[400,384]{1,0:T(8,128)(2,1)S(1)} collective-permute-done((bf16[400,384]{1,0:T(8,128)(2,1)S(1)}, bf16[400,384]{1,0:T(8,128)(2,1)S(1)}, u32[]{:S(2)}, u32[]{:S(2)}) %collective-permute-start.27) | collective-permute-done | bytes 307232 | tf_op jit(solution)/shard_map/ppermute | solution.py:66
  157.5 2.5 %collective-permute-start.28 = (f32[48,384]{1,0:T(8,128)S(1)}, f32[48,384]{1,0:T(8,128)S(1)}, u32[]{:S(2)}, u32[]{:S(2)}) collective-permute-start(f32[48,384]{1,0:T(8,128)S(1)} %get-tuple-element.93), channel_id=1, source_target_pairs={{0,3},{1,0},{2,1},{3,2},{4,7},{5,4},{6,5},{7,6},{8,11},{9,8},{10,9... | collective-permute-start | bytes 221192 | tf_op jit(solution)/shard_map/ppermute | solution.py:42
  160.0 2.2 %collective-permute-start.29 = (f32[48,384]{1,0:T(8,128)S(1)}, f32[48,384]{1,0:T(8,128)S(1)}, u32[]{:S(2)}, u32[]{:S(2)}) collective-permute-start(f32[48,384]{1,0:T(8,128)S(1)} %get-tuple-element.92), channel_id=1, source_target_pairs={{0,2},{1,3},{2,0},{3,1},{4,6},{5,7},{6,4},{7,5},{8,10},{9,11},{10,... | collective-permute-start | bytes 221192 | tf_op jit(solution)/shard_map/ppermute | solution.py:42
  162.9 3.0 %collective-permute-done.29 = f32[48,384]{1,0:T(8,128)S(1)} collective-permute-done((f32[48,384]{1,0:T(8,128)S(1)}, f32[48,384]{1,0:T(8,128)S(1)}, u32[]{:S(2)}, u32[]{:S(2)}) %collective-permute-start.29) | collective-permute-done | bytes 73760 | tf_op jit(solution)/shard_map/ppermute | solution.py:42
  165.9 1.9 %collective-permute-done.30 = f32[48,384]{1,0:T(8,128)S(1)} collective-permute-done((f32[48,384]{1,0:T(8,128)S(1)}, f32[48,384]{1,0:T(8,128)S(1)}, u32[]{:S(2)}, u32[]{:S(2)}) %collective-permute-start.30) | collective-permute-done | bytes 73760 | tf_op jit(solution)/shard_map/ppermute | solution.py:42
  168.4 1.1 broadcast_in_dim_reshape.3
  (149 shorter events, 26.0 us)
Async XLA Ops:
  3.1 5.6 %collective-permute-start = (f32[54,96]{1,0:T(8,128)S(1)}, f32[54,96]{1,0:T(8,128)S(1)}, u32[]{:S(2)}, u32[]{:S(2)}) collective-permute-start(f32[54,96]{1,0:T(8,128)S(1)} %maximum_maximum_fusion), channel_id=1, source_target_pairs={{0,4},{1,5},{2,6},{3,7},{4,0},{5,1},{6,2},{7,3},{8,12},{9,13},{10,... | collective-permute-start | bytes 62216 | tf_op jit(solution)/shard_map/ppermute | solution.py:47
  8.5 8.6 %copy-start.23 = (f32[1,192]{1,0:T(1,128)S(1)}, f32[1,192]{1,0:T(1,128)}, u32[]{:S(2)}) copy-start(f32[1,192]{1,0:T(1,128)} %param.17) | copy-start | bytes 2308
  9.0 13.0 %collective-permute-start.1 = (bf16[408,384]{1,0:T(8,128)(2,1)S(1)}, bf16[408,384]{1,0:T(8,128)(2,1)S(1)}, u32[]{:S(2)}, u32[]{:S(2)}) collective-permute-start(bf16[408,384]{1,0:T(8,128)(2,1)S(1)} %get-tuple-element.104), channel_id=1, source_target_pairs={{0,3},{1,0},{2,1},{3,2},{4,7},{5,4},{6,5},{7,6},{8,11},{9,8},{10,9... | collective-permute-start | bytes 940040 | tf_op jit(solution)/shard_map/ppermute | solution.py:42
  10.9 26.1 %copy-start.12 = (f32[1,192,384]{2,1,0:T(8,128)S(1)}, f32[1,192,384]{2,1,0:T(8,128)}, u32[]{:S(2)}) copy-start(f32[1,192,384]{2,1,0:T(8,128)} %param.18) | copy-start | bytes 884740
  10.9 40.3 %collective-permute-start.5 = (bf16[256,384]{1,0:T(8,128)(2,1)}, bf16[256,384]{1,0:T(8,128)(2,1)}, u32[]{:S(2)}, u32[]{:S(2)}) collective-permute-start(bf16[256,384]{1,0:T(8,128)(2,1)} %bitcast.20.c0), channel_id=1, source_target_pairs={{0,1},{1,2},{2,3},{3,0},{4,5},{5,6},{6,7},{7,4},{8,9},{9,10},{10,1... | collective-permute-start | bytes 589832 | tf_op jit(solution)/shard_map/ppermute | solution.py:42
  11.9 39.3 %collective-permute-start.6 = (bf16[256,384]{1,0:T(8,128)(2,1)}, bf16[256,384]{1,0:T(8,128)(2,1)}, u32[]{:S(2)}, u32[]{:S(2)}) collective-permute-start(bf16[256,384]{1,0:T(8,128)(2,1)} %bitcast.20.c0), channel_id=1, source_target_pairs={{0,2},{1,3},{2,0},{3,1},{4,6},{5,7},{6,4},{7,5},{8,10},{9,11},{10,... | collective-permute-start | bytes 589832 | tf_op jit(solution)/shard_map/ppermute | solution.py:42
  13.2 38.0 %collective-permute-start.7 = (bf16[256,384]{1,0:T(8,128)(2,1)}, bf16[256,384]{1,0:T(8,128)(2,1)}, u32[]{:S(2)}, u32[]{:S(2)}) collective-permute-start(bf16[256,384]{1,0:T(8,128)(2,1)} %bitcast.20.c0), channel_id=1, source_target_pairs={{0,3},{1,0},{2,1},{3,2},{4,7},{5,4},{6,5},{7,6},{8,11},{9,8},{10,9... | collective-permute-start | bytes 589832 | tf_op jit(solution)/shard_map/ppermute | solution.py:42
  14.6 15.6 %collective-permute-start.2 = (bf16[408,384]{1,0:T(8,128)(2,1)S(1)}, bf16[408,384]{1,0:T(8,128)(2,1)S(1)}, u32[]{:S(2)}, u32[]{:S(2)}) collective-permute-start(bf16[408,384]{1,0:T(8,128)(2,1)S(1)} %get-tuple-element.103), channel_id=1, source_target_pairs={{0,2},{1,3},{2,0},{3,1},{4,6},{5,7},{6,4},{7,5},{8,10},{9,11},{10,... | collective-permute-start | bytes 940040 | tf_op jit(solution)/shard_map/ppermute | solution.py:42
  22.0 19.5 %copy-start = (bf16[408,384]{1,0:T(8,128)(2,1)}, bf16[408,384]{1,0:T(8,128)(2,1)S(1)}, u32[]{:S(2)}) copy-start(bf16[408,384]{1,0:T(8,128)(2,1)S(1)} %collective-permute-done.1.i3.refs_3_) | copy-start | bytes 940036
  22.0 14.1 %collective-permute-start.3 = (bf16[408,384]{1,0:T(8,128)(2,1)S(1)}, bf16[408,384]{1,0:T(8,128)(2,1)S(1)}, u32[]{:S(2)}, u32[]{:S(2)}) collective-permute-start(bf16[408,384]{1,0:T(8,128)(2,1)S(1)} %get-tuple-element.102), channel_id=1, source_target_pairs={{0,1},{1,2},{2,3},{3,0},{4,5},{5,6},{6,7},{7,4},{8,9},{9,10},{10,1... | collective-permute-start | bytes 940040 | tf_op jit(solution)/shard_map/ppermute | solution.py:42
  30.2 11.4 %copy-start.2 = (bf16[408,384]{1,0:T(8,128)(2,1)}, bf16[408,384]{1,0:T(8,128)(2,1)S(1)}, u32[]{:S(2)}) copy-start(bf16[408,384]{1,0:T(8,128)(2,1)S(1)} %collective-permute-done.2.i2.refs_2_) | copy-start | bytes 940036
  37.9 12.5 %collective-permute-start.4 = (bf16[400,384]{1,0:T(8,128)(2,1)}, bf16[400,384]{1,0:T(8,128)(2,1)}, u32[]{:S(2)}, u32[]{:S(2)}) collective-permute-start(bf16[400,384]{1,0:T(8,128)(2,1)} %fusion.2.own), channel_id=1, source_target_pairs={{0,4},{1,5},{2,6},{3,7},{4,0},{5,1},{6,2},{7,3},{8,12},{9,13},{10,... | collective-permute-start | bytes 921608 | tf_op jit(solution)/shard_map/ppermute | solution.py:47
  51.2 7.0 %copy-start.24 = (f32[1,192]{1,0:T(1,128)S(1)}, f32[1,192]{1,0:T(1,128)}, u32[]{:S(2)}) copy-start(f32[1,192]{1,0:T(1,128)} %param.22) | copy-start | bytes 2308
  57.8 15.4 %collective-permute-start.17 = (bf16[400,384]{1,0:T(8,128)(2,1)}, bf16[400,384]{1,0:T(8,128)(2,1)}, u32[]{:S(2)}, u32[]{:S(2)}) collective-permute-start(bf16[400,384]{1,0:T(8,128)(2,1)} %get-tuple-element.33), channel_id=1, source_target_pairs={{0,4},{1,5},{2,6},{3,7},{4,0},{5,1},{6,2},{7,3},{8,12},{9,13},{10,... | collective-permute-start | bytes 921608 | tf_op jit(solution)/shard_map/ppermute | solution.py:47
  63.3 9.9 %copy-start.7 = (f32[400,384]{1,0:T(8,128)S(1)}, f32[400,384]{1,0:T(8,128)}, u32[]{:S(2)}) copy-start(f32[400,384]{1,0:T(8,128)} %copy-done.6) | copy-start | bytes 1843204
  63.3 9.9 %copy-start.11 = (f32[4,48,384]{2,1,0:T(8,128)S(1)}, f32[4,48,384]{2,1,0:T(8,128)}, u32[]{:S(2)}) copy-start(f32[4,48,384]{2,1,0:T(8,128)} %copy-done.10) | copy-start | bytes 884740
  63.3 9.9 %copy-start.13 = (f32[1,192,384]{2,1,0:T(8,128)S(1)}, f32[1,192,384]{2,1,0:T(8,128)}, u32[]{:S(2)}) copy-start(f32[1,192,384]{2,1,0:T(8,128)} %param.18) | copy-start | bytes 884740
  63.3 9.9 %copy-start.17 = (f32[4,48,384]{2,1,0:T(8,128)S(1)}, f32[4,48,384]{2,1,0:T(8,128)}, u32[]{:S(2)}) copy-start(f32[4,48,384]{2,1,0:T(8,128)} %get-tuple-element.82) | copy-start | bytes 884740
  63.3 9.9 %copy-start.21 = (f32[1,192,384]{2,1,0:T(8,128)S(1)}, f32[1,192,384]{2,1,0:T(8,128)}, u32[]{:S(2)}) copy-start(f32[1,192,384]{2,1,0:T(8,128)} %param.23) | copy-start | bytes 884740
  70.9 4.4 %collective-permute-start.10 = (bf16[56,384]{1,0:T(8,128)(2,1)S(1)}, bf16[56,384]{1,0:T(8,128)(2,1)S(1)}, u32[]{:S(2)}, u32[]{:S(2)}) collective-permute-start(bf16[56,384]{1,0:T(8,128)(2,1)S(1)} %back.3), channel_id=1, source_target_pairs={{0,3},{1,0},{2,1},{3,2},{4,7},{5,4},{6,5},{7,6},{8,11},{9,8},{10,9... | collective-permute-start | bytes 129032 | tf_op jit(solution)/shard_map/ppermute | solution.py:42
  71.0 5.5 %collective-permute-start.8 = (bf16[56,384]{1,0:T(8,128)(2,1)S(1)}, bf16[56,384]{1,0:T(8,128)(2,1)S(1)}, u32[]{:S(2)}, u32[]{:S(2)}) collective-permute-start(bf16[56,384]{1,0:T(8,128)(2,1)S(1)} %back.3), channel_id=1, source_target_pairs={{0,1},{1,2},{2,3},{3,0},{4,5},{5,6},{6,7},{7,4},{8,9},{9,10},{10,1... | collective-permute-start | bytes 129032 | tf_op jit(solution)/shard_map/ppermute | solution.py:42
  73.0 5.5 %collective-permute-start.9 = (bf16[56,384]{1,0:T(8,128)(2,1)S(1)}, bf16[56,384]{1,0:T(8,128)(2,1)S(1)}, u32[]{:S(2)}, u32[]{:S(2)}) collective-permute-start(bf16[56,384]{1,0:T(8,128)(2,1)S(1)} %back.3), channel_id=1, source_target_pairs={{0,2},{1,3},{2,0},{3,1},{4,6},{5,7},{6,4},{7,5},{8,10},{9,11},{10,... | collective-permute-start | bytes 129032 | tf_op jit(solution)/shard_map/ppermute | solution.py:42
  73.3 7.0 %copy-start.16 = (bf16[1,1,1,8,32,384]{5,4,3,2,1,0:T(8,128)(2,1)S(1)}, bf16[1,1,1,8,32,384]{5,4,3,2,1,0:T(8,128)(2,1)}, u32[]{:S(2)}) copy-start(bf16[1,1,1,8,32,384]{5,4,3,2,1,0:T(8,128)(2,1)} %get-tuple-element.90) | copy-start | bytes 589828
  74.5 11.2 %collective-permute-start.18 = (bf16[400,384]{1,0:T(8,128)(2,1)S(1)}, bf16[400,384]{1,0:T(8,128)(2,1)S(1)}, u32[]{:S(2)}, u32[]{:S(2)}) collective-permute-start(bf16[400,384]{1,0:T(8,128)(2,1)S(1)} %get-tuple-element.76), channel_id=1, source_target_pairs={{248,0},{0,8},{8,16},{16,24},{24,32},{32,40},{40,48},{48,56},{56,6... | collective-permute-start | bytes 921608 | tf_op jit(solution)/shard_map/ppermute | solution.py:66
  78.6 4.6 %collective-permute-start.11 = (bf16[56,384]{1,0:T(8,128)(2,1)S(1)}, bf16[56,384]{1,0:T(8,128)(2,1)S(1)}, u32[]{:S(2)}, u32[]{:S(2)}) collective-permute-start(bf16[56,384]{1,0:T(8,128)(2,1)S(1)} %get-tuple-element.79), channel_id=1, source_target_pairs={{0,4},{1,5},{2,6},{3,7},{4,0},{5,1},{6,2},{7,3},{8,12},{9,13},{10,... | collective-permute-start | bytes 129032 | tf_op jit(solution)/shard_map/ppermute | solution.py:47
  80.3 13.6 %collective-permute-start.14 = (bf16[512,384]{1,0:T(8,128)(2,1)S(1)}, bf16[512,384]{1,0:T(8,128)(2,1)S(1)}, u32[]{:S(2)}, u32[]{:S(2)}) collective-permute-start(bf16[512,384]{1,0:T(8,128)(2,1)S(1)} %pad_maximum_fusion.i0.c0.refs_0_), channel_id=1, source_target_pairs={{0,2},{1,3},{2,0},{3,1},{4,6},{5,7},{6,4},{7,5},{8,10},{9,11},{10,... | collective-permute-start | bytes 1179656 | tf_op jit(solution)/shard_map/ppermute | solution.py:42
  81.0 19.0 %collective-permute-start.15 = (bf16[512,384]{1,0:T(8,128)(2,1)S(1)}, bf16[512,384]{1,0:T(8,128)(2,1)S(1)}, u32[]{:S(2)}, u32[]{:S(2)}) collective-permute-start(bf16[512,384]{1,0:T(8,128)(2,1)S(1)} %pad_maximum_fusion.i0.c0.refs_0_), channel_id=1, source_target_pairs={{0,3},{1,0},{2,1},{3,2},{4,7},{5,4},{6,5},{7,6},{8,11},{9,8},{10,9... | collective-permute-start | bytes 1179656 | tf_op jit(solution)/shard_map/ppermute | solution.py:42
  83.0 17.4 %collective-permute-start.16 = (bf16[512,384]{1,0:T(8,128)(2,1)S(1)}, bf16[512,384]{1,0:T(8,128)(2,1)S(1)}, u32[]{:S(2)}, u32[]{:S(2)}) collective-permute-start(bf16[512,384]{1,0:T(8,128)(2,1)S(1)} %pad_maximum_fusion.i0.c0.refs_0_), channel_id=1, source_target_pairs={{0,1},{1,2},{2,3},{3,0},{4,5},{5,6},{6,7},{7,4},{8,9},{9,10},{10,1... | collective-permute-start | bytes 1179656 | tf_op jit(solution)/shard_map/ppermute | solution.py:42
  83.2 8.2 %collective-permute-start.13 = (bf16[56,384]{1,0:T(8,128)(2,1)S(1)}, bf16[56,384]{1,0:T(8,128)(2,1)S(1)}, u32[]{:S(2)}, u32[]{:S(2)}) collective-permute-start(bf16[56,384]{1,0:T(8,128)(2,1)S(1)} %get-tuple-element.79), channel_id=1, source_target_pairs={{252,0},{253,1},{254,2},{255,3},{248,4},{249,5},{250,6},{251,7},{4... | collective-permute-start | bytes 129032 | tf_op jit(solution)/shard_map/ppermute | solution.py:61
  85.6 7.6 %collective-permute-start.12 = (f32[56,384]{1,0:T(8,128)S(1)}, f32[56,384]{1,0:T(8,128)S(1)}, u32[]{:S(2)}, u32[]{:S(2)}) collective-permute-start(f32[56,384]{1,0:T(8,128)S(1)} %get-tuple-element.78), channel_id=1, source_target_pairs={{248,0},{249,1},{250,2},{251,3},{252,4},{253,5},{254,6},{255,7},{0... | collective-permute-start | bytes 258056 | tf_op jit(solution)/shard_map/ppermute | solution.py:61
  86.8 21.7 %copy-start.14 = (f32[400,384]{1,0:T(8,128)}, f32[400,384]{1,0:T(8,128)S(1)}, u32[]{:S(2)}) copy-start(f32[400,384]{1,0:T(8,128)S(1)} %get-tuple-element.75) | copy-start | bytes 1843204
  91.3 17.2 %collective-permute-start.19 = (bf16[400,384]{1,0:T(8,128)(2,1)S(1)}, bf16[400,384]{1,0:T(8,128)(2,1)S(1)}, u32[]{:S(2)}, u32[]{:S(2)}) collective-permute-start(bf16[400,384]{1,0:T(8,128)(2,1)S(1)} %get-tuple-element.74.own), channel_id=1, source_target_pairs={{0,4},{1,5},{2,6},{3,7},{4,0},{5,1},{6,2},{7,3},{8,12},{9,13},{10,... | collective-permute-start | bytes 921608 | tf_op jit(solution)/shard_map/ppermute | solution.py:47
  117.8 9.0 %copy-start.19 = (f32[1,56,2,4,48]{1,4,3,2,0:T(8,128)S(1)}, f32[1,56,2,4,48]{1,4,3,2,0:T(8,128)}, u32[]{:S(2)}) copy-start(f32[1,56,2,4,48]{1,4,3,2,0:T(8,128)} %get-tuple-element.84) | copy-start | bytes 258052
  121.7 24.2 %copy-start.15 = (f32[400,384]{1,0:T(8,128)S(1)}, f32[400,384]{1,0:T(8,128)}, u32[]{:S(2)}) copy-start(f32[400,384]{1,0:T(8,128)} %copy-done.14) | copy-start | bytes 1843204
  121.7 5.8 %collective-permute-start.20 = (bf16[56,384]{1,0:T(8,128)(2,1)S(1)}, bf16[56,384]{1,0:T(8,128)(2,1)S(1)}, u32[]{:S(2)}, u32[]{:S(2)}) collective-permute-start(bf16[56,384]{1,0:T(8,128)(2,1)S(1)} %back.5), channel_id=1, source_target_pairs={{0,1},{1,2},{2,3},{3,0},{4,5},{5,6},{6,7},{7,4},{8,9},{9,10},{10,1... | collective-permute-start | bytes 129032 | tf_op jit(solution)/shard_map/ppermute | solution.py:42
  123.0 5.5 %collective-permute-start.21 = (bf16[56,384]{1,0:T(8,128)(2,1)S(1)}, bf16[56,384]{1,0:T(8,128)(2,1)S(1)}, u32[]{:S(2)}, u32[]{:S(2)}) collective-permute-start(bf16[56,384]{1,0:T(8,128)(2,1)S(1)} %back.5), channel_id=1, source_target_pairs={{0,2},{1,3},{2,0},{3,1},{4,6},{5,7},{6,4},{7,5},{8,10},{9,11},{10,... | collective-permute-start | bytes 129032 | tf_op jit(solution)/shard_map/ppermute | solution.py:42
  125.4 4.0 %collective-permute-start.22 = (bf16[56,384]{1,0:T(8,128)(2,1)S(1)}, bf16[56,384]{1,0:T(8,128)(2,1)S(1)}, u32[]{:S(2)}, u32[]{:S(2)}) collective-permute-start(bf16[56,384]{1,0:T(8,128)(2,1)S(1)} %back.5), channel_id=1, source_target_pairs={{0,3},{1,0},{2,1},{3,2},{4,7},{5,4},{6,5},{7,6},{8,11},{9,8},{10,9... | collective-permute-start | bytes 129032 | tf_op jit(solution)/shard_map/ppermute | solution.py:42
  129.4 8.6 %collective-permute-start.23 = (bf16[56,384]{1,0:T(8,128)(2,1)S(1)}, bf16[56,384]{1,0:T(8,128)(2,1)S(1)}, u32[]{:S(2)}, u32[]{:S(2)}) collective-permute-start(bf16[56,384]{1,0:T(8,128)(2,1)S(1)} %get-tuple-element.71), channel_id=1, source_target_pairs={{0,4},{1,5},{2,6},{3,7},{4,0},{5,1},{6,2},{7,3},{8,12},{9,13},{10,... | collective-permute-start | bytes 129032 | tf_op jit(solution)/shard_map/ppermute | solution.py:47
  129.8 9.0 %collective-permute-start.25 = (bf16[56,384]{1,0:T(8,128)(2,1)S(1)}, bf16[56,384]{1,0:T(8,128)(2,1)S(1)}, u32[]{:S(2)}, u32[]{:S(2)}) collective-permute-start(bf16[56,384]{1,0:T(8,128)(2,1)S(1)} %get-tuple-element.71), channel_id=1, source_target_pairs={{244,0},{245,1},{246,2},{247,3},{240,4},{241,5},{242,6},{243,7},{2... | collective-permute-start | bytes 129032 | tf_op jit(solution)/shard_map/ppermute | solution.py:61
  131.5 8.2 %collective-permute-start.24 = (f32[56,384]{1,0:T(8,128)S(1)}, f32[56,384]{1,0:T(8,128)S(1)}, u32[]{:S(2)}, u32[]{:S(2)}) collective-permute-start(f32[56,384]{1,0:T(8,128)S(1)} %get-tuple-element.72), channel_id=1, source_target_pairs={{240,0},{241,1},{242,2},{243,3},{244,4},{245,5},{246,6},{247,7},{2... | collective-permute-start | bytes 258056 | tf_op jit(solution)/shard_map/ppermute | solution.py:61
  135.1 14.3 %collective-permute-start.31 = (bf16[256,384]{1,0:T(8,128)(2,1)}, bf16[256,384]{1,0:T(8,128)(2,1)S(1)}, u32[]{:S(2)}, u32[]{:S(2)}) collective-permute-start(bf16[256,384]{1,0:T(8,128)(2,1)} %get-tuple-element.39), channel_id=1, source_target_pairs={{0,3},{1,0},{2,1},{3,2},{4,7},{5,4},{6,5},{7,6},{8,11},{9,8},{10,9... | collective-permute-start | bytes 589832 | tf_op jit(solution)/shard_map/ppermute | solution.py:42
  137.9 11.5 %collective-permute-start.32 = (bf16[256,384]{1,0:T(8,128)(2,1)}, bf16[256,384]{1,0:T(8,128)(2,1)}, u32[]{:S(2)}, u32[]{:S(2)}) collective-permute-start(bf16[256,384]{1,0:T(8,128)(2,1)} %get-tuple-element.40), channel_id=1, source_target_pairs={{0,2},{1,3},{2,0},{3,1},{4,6},{5,7},{6,4},{7,5},{8,10},{9,11},{10,... | collective-permute-start | bytes 589832 | tf_op jit(solution)/shard_map/ppermute | solution.py:42
  138.0 11.4 %collective-permute-start.33 = (bf16[256,384]{1,0:T(8,128)(2,1)}, bf16[256,384]{1,0:T(8,128)(2,1)}, u32[]{:S(2)}, u32[]{:S(2)}) collective-permute-start(bf16[256,384]{1,0:T(8,128)(2,1)} %get-tuple-element.41), channel_id=1, source_target_pairs={{0,1},{1,2},{2,3},{3,0},{4,5},{5,6},{6,7},{7,4},{8,9},{9,10},{10,1... | collective-permute-start | bytes 589832 | tf_op jit(solution)/shard_map/ppermute | solution.py:42
  138.8 7.1 %collective-permute-start.26 = (bf16[400,384]{1,0:T(8,128)(2,1)}, bf16[400,384]{1,0:T(8,128)(2,1)S(1)}, u32[]{:S(2)}, u32[]{:S(2)}) collective-permute-start(bf16[400,384]{1,0:T(8,128)(2,1)} %get-tuple-element.37), channel_id=1, source_target_pairs={{0,4},{1,5},{2,6},{3,7},{4,0},{5,1},{6,2},{7,3},{8,12},{9,13},{10,... | collective-permute-start | bytes 921608 | tf_op jit(solution)/shard_map/ppermute | solution.py:47
  146.1 10.5 %collective-permute-start.27 = (bf16[400,384]{1,0:T(8,128)(2,1)S(1)}, bf16[400,384]{1,0:T(8,128)(2,1)S(1)}, u32[]{:S(2)}, u32[]{:S(2)}) collective-permute-start(bf16[400,384]{1,0:T(8,128)(2,1)S(1)} %get-tuple-element.68), channel_id=1, source_target_pairs={{240,0},{248,8},{0,16},{8,24},{16,32},{24,40},{32,48},{40,56},{48,... | collective-permute-start | bytes 921608 | tf_op jit(solution)/shard_map/ppermute | solution.py:66
  157.5 5.3 %collective-permute-start.28 = (f32[48,384]{1,0:T(8,128)S(1)}, f32[48,384]{1,0:T(8,128)S(1)}, u32[]{:S(2)}, u32[]{:S(2)}) collective-permute-start(f32[48,384]{1,0:T(8,128)S(1)} %get-tuple-element.93), channel_id=1, source_target_pairs={{0,3},{1,0},{2,1},{3,2},{4,7},{5,4},{6,5},{7,6},{8,11},{9,8},{10,9... | collective-permute-start | bytes 221192 | tf_op jit(solution)/shard_map/ppermute | solution.py:42
  160.0 5.9 %collective-permute-start.29 = (f32[48,384]{1,0:T(8,128)S(1)}, f32[48,384]{1,0:T(8,128)S(1)}, u32[]{:S(2)}, u32[]{:S(2)}) collective-permute-start(f32[48,384]{1,0:T(8,128)S(1)} %get-tuple-element.92), channel_id=1, source_target_pairs={{0,2},{1,3},{2,0},{3,1},{4,6},{5,7},{6,4},{7,5},{8,10},{9,11},{10,... | collective-permute-start | bytes 221192 | tf_op jit(solution)/shard_map/ppermute | solution.py:42
  162.2 5.6 %collective-permute-start.30 = (f32[48,384]{1,0:T(8,128)S(1)}, f32[48,384]{1,0:T(8,128)S(1)}, u32[]{:S(2)}, u32[]{:S(2)}) collective-permute-start(f32[48,384]{1,0:T(8,128)S(1)} %get-tuple-element.91), channel_id=1, source_target_pairs={{0,1},{1,2},{2,3},{3,0},{4,5},{5,6},{6,7},{7,4},{8,9},{9,10},{10,1... | collective-permute-start | bytes 221192 | tf_op jit(solution)/shard_map/ppermute | solution.py:42
  (11 other events, 26.8 us)
